TPU v7x, 512 devices: a whole 4x8x8 slice. The times are simulated.
512 devices in a mesh: tile: 64 (over z, x, core), blk: 8 (over y).
Axes of the slice: x: 4, y: 8, z: 8, core: 2. Of those that a mesh axis runs over, the one named last changes fastest.
Arguments:
- ensemble: float32 [8, 5, 64, 256, 128], P('blk', None, None, 'tile'), may hold values from -6 to 6
- obs_col: int32 [13312], P('tile'), may hold values from 0 to 255, as said below
- obs_row: int32 [13312], P('tile'), may hold values from 0 to 127
- obs_level: int32 [13312], P('tile'), may hold values from 0 to 7
- obs_field: int32 [13312], P('tile'), may hold values from 0 to 4
- obs_batch: int32 [13312], P('tile'), may hold values from 0 to 3
- obs_value: float32 [13312], P('tile'), may hold values from -8 to 8
- obs_error: float32 [13312], P('tile'), may hold values from 0.3 to 3
- band_reach: int32 [8], replicated, may hold values from 1 to 6
Outputs:
- analysis: float32 [8, 5, 64, 256, 128], P('blk', None, None, 'tile')
Inputs may be any that keep to these rules, and one draw needn't show every extreme that they name: `obs_col`: observation i lies in the strip of the tile that holds it: columns (i // 208) * 4 to (i // 208) * 4 + 3.
All inputs are finite; a program needn't handle non-finite values.
Results may differ from a plain program's by a relative error of at most 0.0003.
Values sent between devices are 32-bit elements; how exact they have to be, the bound alone decides.
A program may use at most 64 MiB of HBM per device.

v0:
```python
import jax
import jax.numpy as jnp
from jax import lax
from jax.sharding import PartitionSpec as P

NBATCH = 4


def padded(x, sides, width):
    for axis, dim in sides:
        size, length = (lax.axis_size(axis), x.shape[dim])
        up = [(i, (i + 1) % size) for i in range(size - 1)]
        down = [(j, i) for i, j in up]
        last = lax.slice_in_dim(x, length - width, length, axis=dim)
        leading = lax.slice_in_dim(x, 0, width, axis=dim)
        before = lax.ppermute(last, axis, up)
        after = lax.ppermute(leading, axis, down)
        x = jnp.concatenate([before, x, after], axis=dim)
    return x


def horizontal(src_col, src_row, dst_col, dst_row, radius):
    col_gap = (src_col[:, None] - dst_col[None, :]).astype(jnp.float32)
    row_gap = (src_row[:, None] - dst_row[None, :]).astype(jnp.float32)
    closeness = 1.0 - (col_gap * col_gap + row_gap * row_gap) / jnp.float32(radius * radius)
    return jnp.square(jnp.maximum(closeness, 0.0))


def batch_stats(near_priors, near_values, plus_batch, batch_turn):
    members = near_priors.shape[0]
    average = jnp.mean(near_priors, axis=0)
    deviation = near_priors - average
    valid = plus_batch > 0
    active = plus_batch == batch_turn + 1
    error_var = jnp.where(valid, near_values[1], jnp.float32(1.0))
    total = jnp.sum(deviation * deviation, axis=0) / (members - 1) + error_var
    shrink = 1.0 / (1.0 + jnp.sqrt(error_var / total))
    innovation = near_values[0] - average
    coefficient = jnp.where(active, 1.0 / (total * (members - 1)), jnp.float32(0.0))
    return (deviation, innovation, coefficient, shrink)


def gain_apply(deviation, innovation, coefficient, shrink, taper, members):
    average = jnp.mean(members, axis=0)
    spread = members - average
    covariance = lax.dot_general(
        deviation,
        spread,
        (((0,), (0,)), ((), ())),
        precision=lax.Precision.HIGHEST,
        preferred_element_type=jnp.float32,
    )
    gain = covariance * taper * coefficient[:, None]
    average = average + jnp.dot(
        innovation, gain, precision=lax.Precision.HIGHEST, preferred_element_type=jnp.float32
    )
    spread = spread - jnp.dot(
        deviation * shrink,
        gain,
        precision=lax.Precision.HIGHEST,
        preferred_element_type=jnp.float32,
    )
    return average + spread


def update_state(state, stats, near_level, taper_flat, reach_here, first_level, fields):
    deviation, innovation, coefficient, shrink = stats

    def one_slab(inputs):
        slab, slab_index = inputs
        level = first_level + slab_index // fields
        reach_level = reach_here[slab_index // fields]
        vertical = jnp.maximum(
            0.0,
            1.0
            - jnp.abs(level - near_level).astype(jnp.float32)
            / (reach_level + 1).astype(jnp.float32),
        )
        return gain_apply(deviation, innovation, coefficient * vertical, shrink, taper_flat, slab)

    return lax.map(one_slab, (state, jnp.arange(state.shape[0], dtype=jnp.int32)))


def update_obs(own_priors, stats, near_places, own_places, band_reach, radius):
    deviation, innovation, coefficient, shrink = stats
    taper_obs = horizontal(near_places[0], near_places[1], own_places[0], own_places[1], radius)
    own_level = own_places[2]
    level_count = band_reach.shape[0]
    match = own_level[None, :] == jnp.arange(level_count, dtype=jnp.int32)[:, None]
    reach_own = jnp.sum(jnp.where(match, band_reach[:, None], 0), axis=0)
    vertical = jnp.maximum(
        0.0,
        1.0
        - jnp.abs(own_level[None, :] - near_places[2][:, None]).astype(jnp.float32)
        / (reach_own[None, :] + 1).astype(jnp.float32),
    )
    return gain_apply(deviation, innovation, coefficient, shrink, taper_obs * vertical, own_priors)


def shards(
    ensemble, obs_col, obs_row, obs_level, obs_field, obs_batch, obs_value, obs_error, band_reach
):
    lev_dev, fields, members, strip_cols, grid_rows = ensemble.shape
    obs_count = obs_col.shape[0]
    tile_index = lax.axis_index("tile")
    block_index = lax.axis_index("blk")
    first_level = block_index * lev_dev
    places = jnp.stack([obs_col, obs_row, obs_level, obs_field, obs_batch + 1])
    near_places = padded(places, (("tile", 1),), obs_count)
    values = jnp.stack([obs_value, obs_error])
    near_values = padded(values, (("tile", 1),), obs_count)
    state = ensemble.reshape(lev_dev * fields, members, strip_cols * grid_rows)
    cells = jnp.arange(strip_cols * grid_rows, dtype=jnp.int32)
    cell_col = tile_index * strip_cols + cells // grid_rows
    cell_row = cells % grid_rows
    local_cell = (obs_col - tile_index * strip_cols) * grid_rows + obs_row
    picked = jnp.take(state, local_cell, axis=2)
    slot_index = (obs_level - first_level) * fields + obs_field
    select = (jnp.arange(lev_dev * fields, dtype=jnp.int32)[:, None] == slot_index[None, :]).astype(
        jnp.float32
    )
    extracted = jnp.sum(picked * select[:, None, :], axis=0)
    taper_flat = horizontal(near_places[0], near_places[1], cell_col, cell_row, strip_cols)
    reach_here = lax.dynamic_slice_in_dim(band_reach, first_level, lev_dev)
    priors = lax.psum(extracted, "blk")
    for batch_turn in range(NBATCH):
        near_priors = padded(priors, (("tile", 1),), obs_count)
        stats = batch_stats(near_priors, near_values, near_places[4], batch_turn)
        state = update_state(
            state, stats, near_places[2], taper_flat, reach_here, first_level, fields
        )
        if batch_turn + 1 < NBATCH:
            priors = update_obs(priors, stats, near_places, places, band_reach, strip_cols)
    return state.reshape(lev_dev, fields, members, strip_cols, grid_rows)


def solution(mesh):
    return jax.shard_map(
        shards,
        mesh=mesh,
        in_specs=(
            P("blk", None, None, "tile", None),
            P("tile"),
            P("tile"),
            P("tile"),
            P("tile"),
            P("tile"),
            P("tile"),
            P("tile"),
            P(),
        ),
        out_specs=P("blk", None, None, "tile", None),
        check_vma=False,
    )
```

profile of v0, /device:TPU:256, one launch (start us, length us, event | category | flops | bytes accessed | tf_op | source)
XLA Modules:
  0.0 221.6 jit_solution(798128900312683574)
XLA Ops:
  1.5 1.8 copy.15
  3.4 0.9 gather_fusion
  4.3 1.2 fusion.58
  5.7 30.8 %psum.7 = f32[64,208]{1,0:T(8,128)S(1)} all-reduce(f32[64,208]{1,0:T(8,128)S(1)} %copy.16), channel_id=1, replica_groups=mesh['tile'=64,'blk'=8] {'blk'}, use_global_device_ids=true, to_apply=%region_1.2 | all-reduce | flops 13312 | bytes 106496 | tf_op jit(solution)/shard_map/psum | solution.py:125
  36.5 1.9 collective-permute-start
  38.4 7.0 %collective-permute-start.1 = (f32[64,208]{1,0:T(8,128)S(1)}, f32[64,208]{1,0:T(8,128)S(1)}, u32[]{:S(2)}, u32[]{:S(2)}) collective-permute-start(f32[64,208]{1,0:T(8,128)S(1)} %psum.7), channel_id=1, source_target_pairs={{8,0},{16,8},{24,16},{32,24},{40,32},{48,40},{56,48},{64,56},{72,6... | collective-permute-start | bytes 159752 | tf_op jit(solution)/shard_map/ppermute | solution.py:17
  45.4 1.9 collective-permute-start.4
  47.3 7.0 %collective-permute-start.5 = (f32[2,208]{1,0:T(2,128)S(1)}, f32[2,208]{1,0:T(2,128)S(1)}, u32[]{:S(2)}, u32[]{:S(2)}) collective-permute-start(f32[2,208]{1,0:T(2,128)S(1)} %pad_maximum_fusion.5), channel_id=1, source_target_pairs={{8,0},{16,8},{24,16},{32,24},{40,32},{48,40},{56,48},{64,56},{72,6... | collective-permute-start | bytes 5000 | tf_op jit(solution)/shard_map/ppermute | solution.py:17
  54.4 1.9 collective-permute-start.2
  58.2 7.0 %collective-permute-start.3 = (s32[5,208]{1,0:T(8,128)S(1)}, s32[5,208]{1,0:T(8,128)S(1)}, u32[]{:S(2)}, u32[]{:S(2)}) collective-permute-start(s32[5,208]{1,0:T(8,128)S(1)} %stack.32), channel_id=1, source_target_pairs={{8,0},{16,8},{24,16},{32,24},{40,32},{48,40},{56,48},{64,56},{72,6... | collective-permute-start | bytes 12488 | tf_op jit(solution)/shard_map/ppermute | solution.py:17
  65.3 1.2 collective-permute-done.3
  69.4 1.9 collective-permute-start.6
  71.4 7.0 %collective-permute-start.7 = (f32[64,208]{1,0:T(8,128)S(1)}, f32[64,208]{1,0:T(8,128)S(1)}, u32[]{:S(2)}, u32[]{:S(2)}) collective-permute-start(f32[64,208]{1,0:T(8,128)S(1)} %get-tuple-element.969), channel_id=1, source_target_pairs={{8,0},{16,8},{24,16},{32,24},{40,32},{48,40},{56,48},{64,56},{72,6... | collective-permute-start | bytes 159752 | tf_op jit(solution)/shard_map/ppermute | solution.py:17
  78.5 30.8 %while.56 = (s32[]{:T(128)}, f32[5,64,512]{2,1,0:T(8,128)S(1)}, f32[5,64,512]{2,1,0:T(8,128)S(1)}, f32[64,624]{1,0:T(8,128)S(1)}, s32[5]{0:T(128)S(1)}, /*index=...) while((s32[]{:T(128)}, f32[5,64,512]{2,1,0:T(8,128)S(1)}, ...), condition=%wide.wide.region_6.7_spmd.clone, body=%wide.wide.region_4.6_spmd.clone.sunk | while | flops 498929952 | bytes 4737079 | solution.py:81
  81.3 1.6 fusion.214
  87.4 1.6 fusion.214
  93.6 1.6 fusion.214
  99.7 1.6 fusion.214
  105.9 1.6 fusion.214
  109.6 0.9 fusion.53
  111.9 1.9 collective-permute-start.8
  113.9 7.1 %collective-permute-start.9 = (f32[64,208]{1,0:T(8,128)S(1)}, f32[64,208]{1,0:T(8,128)S(1)}, u32[]{:S(2)}, u32[]{:S(2)}) collective-permute-start(f32[64,208]{1,0:T(8,128)S(1)} %get-tuple-element.971), channel_id=1, source_target_pairs={{8,0},{16,8},{24,16},{32,24},{40,32},{48,40},{56,48},{64,56},{72,6... | collective-permute-start | bytes 159752 | tf_op jit(solution)/shard_map/ppermute | solution.py:17
  121.1 28.4 %while.57 = (s32[]{:T(128)}, f32[5,64,512]{2,1,0:T(8,128)S(1)}, f32[5,64,512]{2,1,0:T(8,128)S(1)}, f32[64,624]{1,0:T(8,128)S(1)}, s32[5]{0:T(128)S(1)}, /*index=...) while((s32[]{:T(128)}, f32[5,64,512]{2,1,0:T(8,128)S(1)}, ...), condition=%wide.wide.region_13.14_spmd.clone, body=%wide.wide.region_11.13_spmd.clone.sunk | while | flops 498929952 | bytes 4737079 | solution.py:81
  123.5 1.6 fusion.223
  125.9 0.9 fusion.226
  129.1 1.6 fusion.223
  131.5 0.9 fusion.226
  134.8 1.6 fusion.223
  137.2 0.9 fusion.226
  140.5 1.6 fusion.223
  142.9 0.9 fusion.226
  146.2 1.6 fusion.223
  148.6 0.9 fusion.226
  152.2 1.9 collective-permute-start.10
  154.1 7.0 %collective-permute-start.11 = (f32[64,208]{1,0:T(8,128)S(1)}, f32[64,208]{1,0:T(8,128)S(1)}, u32[]{:S(2)}, u32[]{:S(2)}) collective-permute-start(f32[64,208]{1,0:T(8,128)S(1)} %fusion.55), channel_id=1, source_target_pairs={{8,0},{16,8},{24,16},{32,24},{40,32},{48,40},{56,48},{64,56},{72,6... | collective-permute-start | bytes 159752 | tf_op jit(solution)/shard_map/ppermute | solution.py:17
  161.2 29.3 %while.58 = (s32[]{:T(128)}, f32[5,64,512]{2,1,0:T(8,128)S(1)}, f32[5,64,512]{2,1,0:T(8,128)S(1)}, f32[64,624]{1,0:T(8,128)S(1)}, s32[5]{0:T(128)S(1)}, /*index=...) while((s32[]{:T(128)}, f32[5,64,512]{2,1,0:T(8,128)S(1)}, ...), condition=%wide.wide.region_19.20_spmd.clone, body=%wide.wide.region_17.19_spmd.clone.sunk | while | flops 498929952 | bytes 4737079 | solution.py:81
  163.7 1.6 fusion.232
  169.6 1.6 fusion.232
  175.5 1.6 fusion.232
  181.3 1.6 fusion.232
  187.2 1.6 fusion.232
  191.3 29.3 %while.59 = (s32[]{:T(128)}, f32[5,64,512]{2,1,0:T(8,128)S(1)}, f32[5,64,512]{2,1,0:T(8,128)S(1)}, f32[64,624]{1,0:T(8,128)S(1)}, s32[5]{0:T(128)S(1)}, /*index=...) while((s32[]{:T(128)}, f32[5,64,512]{2,1,0:T(8,128)S(1)}, ...), condition=%wide.wide.region_25.26_spmd.clone, body=%wide.wide.region_23.25_spmd.clone.sunk | while | flops 498929952 | bytes 4737079 | solution.py:81
  193.8 1.6 fusion.241
  199.7 1.6 fusion.241
  205.5 1.6 fusion.241
  211.4 1.6 fusion.241
  217.2 1.6 fusion.241
  220.5 1.0 reshape.303
  (236 shorter events, 53.5 us)
Async XLA Ops:
  3.3 42.1 %copy-start.6 = (f32[208]{0:T(256)S(1)}, f32[208]{0:T(256)}, u32[]{:S(2)}) copy-start(f32[208]{0:T(256)} %param.24) | copy-start | bytes 2500
  3.3 42.1 %copy-start.7 = (f32[208]{0:T(256)S(1)}, f32[208]{0:T(256)}, u32[]{:S(2)}) copy-start(f32[208]{0:T(256)} %param.23) | copy-start | bytes 2500
  3.3 51.0 %copy-start.10 = (s32[208]{0:T(256)S(1)}, s32[208]{0:T(256)}, u32[]{:S(2)}) copy-start(s32[208]{0:T(256)} %param.22) | copy-start | bytes 2500
  3.3 51.0 %copy-start.4 = (s32[208]{0:T(256)S(1)}, s32[208]{0:T(256)}, u32[]{:S(2)}) copy-start(s32[208]{0:T(256)} %param.20) | copy-start | bytes 2500
  3.4 51.0 %copy-start.5 = (s32[208]{0:T(256)S(1)}, s32[208]{0:T(256)}, u32[]{:S(2)}) copy-start(s32[208]{0:T(256)} %param.21) | copy-start | bytes 2500
  3.4 51.0 %copy-start.8 = (s32[208]{0:T(256)S(1)}, s32[208]{0:T(256)}, u32[]{:S(2)}) copy-start(s32[208]{0:T(256)} %param.19) | copy-start | bytes 2500
  3.4 51.0 %copy-start.9 = (s32[208]{0:T(256)S(1)}, s32[208]{0:T(256)}, u32[]{:S(2)}) copy-start(s32[208]{0:T(256)} %param.18) | copy-start | bytes 2500
  3.4 53.0 %copy-start.11 = (s32[8]{0:T(128)S(1)}, s32[8]{0:T(128)}, u32[]{:S(2)}) copy-start(s32[8]{0:T(128)} %param.25) | copy-start | bytes 100
  36.5 30.2 %collective-permute-start = (f32[64,208]{1,0:T(8,128)S(1)}, f32[64,208]{1,0:T(8,128)S(1)}, u32[]{:S(2)}, u32[]{:S(2)}) collective-permute-start(f32[64,208]{1,0:T(8,128)S(1)} %psum.7), channel_id=1, source_target_pairs={{0,8},{8,16},{16,24},{24,32},{32,40},{40,48},{48,56},{56,64},{64,7... | collective-permute-start | bytes 159752 | tf_op jit(solution)/shard_map/ppermute | solution.py:16
  38.4 28.3 %collective-permute-start.1 = (f32[64,208]{1,0:T(8,128)S(1)}, f32[64,208]{1,0:T(8,128)S(1)}, u32[]{:S(2)}, u32[]{:S(2)}) collective-permute-start(f32[64,208]{1,0:T(8,128)S(1)} %psum.7), channel_id=1, source_target_pairs={{8,0},{16,8},{24,16},{32,24},{40,32},{48,40},{56,48},{64,56},{72,6... | collective-permute-start | bytes 159752 | tf_op jit(solution)/shard_map/ppermute | solution.py:17
  45.4 12.8 %collective-permute-start.4 = (f32[2,208]{1,0:T(2,128)S(1)}, f32[2,208]{1,0:T(2,128)S(1)}, u32[]{:S(2)}, u32[]{:S(2)}) collective-permute-start(f32[2,208]{1,0:T(2,128)S(1)} %pad_maximum_fusion.5), channel_id=1, source_target_pairs={{0,8},{8,16},{16,24},{24,32},{32,40},{40,48},{48,56},{56,64},{64,7... | collective-permute-start | bytes 5000 | tf_op jit(solution)/shard_map/ppermute | solution.py:16
  47.3 17.9 %collective-permute-start.5 = (f32[2,208]{1,0:T(2,128)S(1)}, f32[2,208]{1,0:T(2,128)S(1)}, u32[]{:S(2)}, u32[]{:S(2)}) collective-permute-start(f32[2,208]{1,0:T(2,128)S(1)} %pad_maximum_fusion.5), channel_id=1, source_target_pairs={{8,0},{16,8},{24,16},{32,24},{40,32},{48,40},{56,48},{64,56},{72,6... | collective-permute-start | bytes 5000 | tf_op jit(solution)/shard_map/ppermute | solution.py:17
  54.4 10.9 %collective-permute-start.2 = (s32[5,208]{1,0:T(8,128)S(1)}, s32[5,208]{1,0:T(8,128)S(1)}, u32[]{:S(2)}, u32[]{:S(2)}) collective-permute-start(s32[5,208]{1,0:T(8,128)S(1)} %stack.32), channel_id=1, source_target_pairs={{0,8},{8,16},{16,24},{24,32},{32,40},{40,48},{48,56},{56,64},{64,7... | collective-permute-start | bytes 12488 | tf_op jit(solution)/shard_map/ppermute | solution.py:16
  58.2 8.3 %collective-permute-start.3 = (s32[5,208]{1,0:T(8,128)S(1)}, s32[5,208]{1,0:T(8,128)S(1)}, u32[]{:S(2)}, u32[]{:S(2)}) collective-permute-start(s32[5,208]{1,0:T(8,128)S(1)} %stack.32), channel_id=1, source_target_pairs={{8,0},{16,8},{24,16},{32,24},{40,32},{48,40},{56,48},{64,56},{72,6... | collective-permute-start | bytes 12488 | tf_op jit(solution)/shard_map/ppermute | solution.py:17
  67.1 11.2 %copy-start.2 = (f32[624]{0:T(1024)}, f32[624]{0:T(1024)S(1)}, u32[]{:S(2)}) copy-start(f32[624]{0:T(1024)S(1)} %get-tuple-element.1612) | copy-start | bytes 7492
  69.4 39.8 %collective-permute-start.6 = (f32[64,208]{1,0:T(8,128)S(1)}, f32[64,208]{1,0:T(8,128)S(1)}, u32[]{:S(2)}, u32[]{:S(2)}) collective-permute-start(f32[64,208]{1,0:T(8,128)S(1)} %get-tuple-element.969), channel_id=1, source_target_pairs={{0,8},{8,16},{16,24},{24,32},{32,40},{40,48},{48,56},{56,64},{64,7... | collective-permute-start | bytes 159752 | tf_op jit(solution)/shard_map/ppermute | solution.py:16
  71.4 37.9 %collective-permute-start.7 = (f32[64,208]{1,0:T(8,128)S(1)}, f32[64,208]{1,0:T(8,128)S(1)}, u32[]{:S(2)}, u32[]{:S(2)}) collective-permute-start(f32[64,208]{1,0:T(8,128)S(1)} %get-tuple-element.969), channel_id=1, source_target_pairs={{8,0},{16,8},{24,16},{32,24},{40,32},{48,40},{56,48},{64,56},{72,6... | collective-permute-start | bytes 159752 | tf_op jit(solution)/shard_map/ppermute | solution.py:17
  109.4 11.6 %copy-start = (f32[624]{0:T(1024)}, f32[624]{0:T(1024)S(1)}, u32[]{:S(2)}) copy-start(f32[624]{0:T(1024)S(1)} %get-tuple-element.1675) | copy-start | bytes 7492
  111.9 37.6 %collective-permute-start.8 = (f32[64,208]{1,0:T(8,128)S(1)}, f32[64,208]{1,0:T(8,128)S(1)}, u32[]{:S(2)}, u32[]{:S(2)}) collective-permute-start(f32[64,208]{1,0:T(8,128)S(1)} %get-tuple-element.971), channel_id=1, source_target_pairs={{0,8},{8,16},{16,24},{24,32},{32,40},{40,48},{48,56},{56,64},{64,7... | collective-permute-start | bytes 159752 | tf_op jit(solution)/shard_map/ppermute | solution.py:16
  113.9 35.7 %collective-permute-start.9 = (f32[64,208]{1,0:T(8,128)S(1)}, f32[64,208]{1,0:T(8,128)S(1)}, u32[]{:S(2)}, u32[]{:S(2)}) collective-permute-start(f32[64,208]{1,0:T(8,128)S(1)} %get-tuple-element.971), channel_id=1, source_target_pairs={{8,0},{16,8},{24,16},{32,24},{40,32},{48,40},{56,48},{64,56},{72,6... | collective-permute-start | bytes 159752 | tf_op jit(solution)/shard_map/ppermute | solution.py:17
  149.7 11.4 %copy-start.1 = (f32[624]{0:T(1024)}, f32[624]{0:T(1024)S(1)}, u32[]{:S(2)}) copy-start(f32[624]{0:T(1024)S(1)} %get-tuple-element.1738) | copy-start | bytes 7492
  152.2 38.4 %collective-permute-start.10 = (f32[64,208]{1,0:T(8,128)S(1)}, f32[64,208]{1,0:T(8,128)S(1)}, u32[]{:S(2)}, u32[]{:S(2)}) collective-permute-start(f32[64,208]{1,0:T(8,128)S(1)} %fusion.55), channel_id=1, source_target_pairs={{0,8},{8,16},{16,24},{24,32},{32,40},{40,48},{48,56},{56,64},{64,7... | collective-permute-start | bytes 159752 | tf_op jit(solution)/shard_map/ppermute | solution.py:16
  154.1 36.4 %collective-permute-start.11 = (f32[64,208]{1,0:T(8,128)S(1)}, f32[64,208]{1,0:T(8,128)S(1)}, u32[]{:S(2)}, u32[]{:S(2)}) collective-permute-start(f32[64,208]{1,0:T(8,128)S(1)} %fusion.55), channel_id=1, source_target_pairs={{8,0},{16,8},{24,16},{32,24},{40,32},{48,40},{56,48},{64,56},{72,6... | collective-permute-start | bytes 159752 | tf_op jit(solution)/shard_map/ppermute | solution.py:17
  190.7 0.6 copy-start.3
where the time goes:
time: 223 us; the launch traced here: 222 us
  matrix products  72.7 us (33%)
  starting transfers between devices  53.5 us (24%)
  loops' own time  38.4 us (17%)
  blocking collectives  30.8 us (14%)
  local copies, waits for them, and re-layouts  17.9 us (8%)
  other arithmetic  5.54 us (2%)
    ppermute x6, starting transfers between devices, padded(): after = lax.ppermute(leading, axis, down)  42 us
    another operation x4, loops' own time, update_state(): lax.map(one_slab, (state, jnp.arange(state.shape[0], dtype=jnp.int32)))  38.4 us
    dot_general x23, matrix products, gain_apply(): lax.dot_general(deviation, spread, (((0,), (0,)), ((), ())), precision=la...  35 us
    psum x1, blocking collectives, shards(): priors = lax.psum(extracted, 'blk')  30.8 us
    dot_general x23, matrix products, gain_apply(): jnp.dot(deviation * shrink, gain, precision=lax.Precision.HIGHEST, prefer...  20.6 us
    dot_general x23, matrix products, gain_apply(): jnp.dot(innovation, gain, precision=lax.Precision.HIGHEST, preferred_elem...  17.1 us
    dynamic_slice x20, local copies, waits for them, and re-layouts, update_state(): lax.map(one_slab, (state, jnp.arange(state.shape[0], dtype=jnp.int32)))  12.3 us
    ppermute x6, starting transfers between devices, padded(): before = lax.ppermute(last, axis, up)  11.5 us
  transfers between devices with their start and end apart: 12, of which 1 were waited for; matrix products, arithmetic and copies ran while one was open for 28% of the time, Pallas kernels for 0%

commit v1 on v0

v1 whole, which is shorter than its diff:
```python
import functools

import jax
import jax.numpy as jnp
from jax import lax
from jax.experimental import pallas as pl
from jax.experimental.pallas import tpu as pltpu
from jax.sharding import PartitionSpec as P

MESH = pl.DeviceIdType.MESH
NBATCH = 4
F32 = jnp.float32
BF16 = jnp.bfloat16
LANES = 128


def split(x):
    high = x.astype(BF16)
    low = (x - high.astype(F32)).astype(BF16)
    return high, low


def dot(a, b):
    return jnp.dot(a, b, preferred_element_type=F32)


def kernel(
    sizes,
    x_hbm,
    col_ref,
    row_ref,
    level_ref,
    field_ref,
    batch_ref,
    value_ref,
    error_ref,
    reach_ref,
    out_ref,
    x_in,
    state,
    near,
    meta,
    taper_state,
    taper_obs,
    picked,
    parts,
    dev_t,
    factor,
    load_sem,
    meta_send,
    meta_recv,
    rs_send,
    rs_recv,
    ag_send,
    ag_recv,
    halo_send,
    halo_recv,
):
    tiles, blocks, fields, members, cols, rows, obs, wide = sizes
    cells = cols * rows
    share = members // blocks
    tile = lax.axis_index("tile")
    level = lax.axis_index("blk")
    has_left, has_right = tile > 0, tile < tiles - 1

    load = pltpu.make_async_copy(x_hbm, x_in, load_sem)
    load.start()

    barrier = pltpu.get_barrier_semaphore()
    for step in range(1, blocks):
        pl.semaphore_signal(
            barrier, inc=1, device_id={"blk": lax.rem(level + step, blocks)}, device_id_type=MESH
        )

    @pl.when(has_left)
    def _():
        pl.semaphore_signal(barrier, inc=1, device_id={"tile": tile - 1}, device_id_type=MESH)

    @pl.when(has_right)
    def _():
        pl.semaphore_signal(barrier, inc=1, device_id={"tile": tile + 1}, device_id_type=MESH)

    meta[1] = jnp.zeros((8, wide), F32)
    meta[1, 0:1, :obs] = col_ref[...].astype(F32)
    meta[1, 1:2, :obs] = row_ref[...].astype(F32)
    meta[1, 2:3, :obs] = level_ref[...].astype(F32)
    meta[1, 3:4, :obs] = field_ref[...].astype(F32)
    meta[1, 4:5, :obs] = (batch_ref[...] + 1).astype(F32)
    meta[1, 5:6, :obs] = value_ref[...]
    meta[1, 6:7, :obs] = error_ref[...]

    @pl.when(jnp.logical_not(has_left))
    def _():
        near[:, 0] = jnp.zeros((NBATCH, members, wide), F32)
        meta[0] = jnp.zeros((8, wide), F32)

    @pl.when(jnp.logical_not(has_right))
    def _():
        near[:, 2] = jnp.zeros((NBATCH, members, wide), F32)
        meta[2] = jnp.zeros((8, wide), F32)

    pl.semaphore_wait(
        barrier, (blocks - 1) + has_left.astype(jnp.int32) + has_right.astype(jnp.int32)
    )

    def strips(array, send, recv):
        right = pltpu.make_async_remote_copy(
            src_ref=array.at[1],
            dst_ref=array.at[0],
            send_sem=send.at[0],
            recv_sem=recv.at[0],
            device_id={"tile": jnp.minimum(tile + 1, tiles - 1)},
            device_id_type=MESH,
        )
        left = pltpu.make_async_remote_copy(
            src_ref=array.at[1],
            dst_ref=array.at[2],
            send_sem=send.at[1],
            recv_sem=recv.at[1],
            device_id={"tile": jnp.maximum(tile - 1, 0)},
            device_id_type=MESH,
        )
        return right, left

    def strips_start(array, send, recv):
        right, left = strips(array, send, recv)
        pl.when(has_right)(right.start)
        pl.when(has_left)(left.start)

    def strips_arrive(array, send, recv):
        right, left = strips(array, send, recv)
        pl.when(has_left)(right.wait_recv)
        pl.when(has_right)(left.wait_recv)

    def strips_sent(array, send, recv):
        right, left = strips(array, send, recv)
        pl.when(has_right)(right.wait_send)
        pl.when(has_left)(left.wait_send)

    strips_start(meta, meta_send, meta_recv)

    own_col, own_row, own_level, own_field = (meta[1, i : i + 1, :] for i in range(4))
    here = (own_level == level.astype(F32)) & (meta[1, 4:5, :] > 0)
    place = (own_field * cols + own_col - (tile * cols).astype(F32)) * rows + own_row
    place = jnp.where(here, place, -1.0)
    load.wait()
    cell_at = lax.broadcasted_iota(jnp.int32, (cells, wide), 0).astype(F32)

    def slab(ref, f):
        return jnp.concatenate(
            [ref[pl.ds(f * members * cols + c, members, stride=cols), :] for c in range(cols)], axis=1
        )

    total = jnp.zeros((3 * members, wide), F32)
    for f in range(fields):
        x = slab(x_in, f)
        high = x.astype(BF16)
        rest = x - high.astype(F32)
        middle, low = split(rest)
        chosen = jnp.where(cell_at + float(f * cells) == place, 1.0, 0.0).astype(BF16)
        total = total + dot(jnp.concatenate([high, middle, low], axis=0), chosen)
    picked[...] = total[:members] + total[members : 2 * members] + total[2 * members :]

    def scatter(step):
        peer = lax.rem(level + step, blocks)
        return pltpu.make_async_remote_copy(
            src_ref=picked.at[pl.ds(pl.multiple_of(peer * share, share), share)],
            dst_ref=parts.at[step],
            send_sem=rs_send.at[step],
            recv_sem=rs_recv.at[step],
            device_id={"blk": peer},
            device_id_type=MESH,
        )

    mine = pl.ds(pl.multiple_of(level * share, share), share)

    def gather(step):
        peer = lax.rem(level + step, blocks)
        return pltpu.make_async_remote_copy(
            src_ref=near.at[0, 1, mine],
            dst_ref=near.at[0, 1, mine],
            send_sem=ag_send.at[step],
            recv_sem=ag_recv.at[step],
            device_id={"blk": peer},
            device_id_type=MESH,
        )

    def gather_arrive(step):
        source = lax.rem(level + blocks - step, blocks)
        at = pl.ds(pl.multiple_of(source * share, share), share)
        pltpu.make_async_remote_copy(
            src_ref=near.at[0, 1, at],
            dst_ref=near.at[0, 1, at],
            send_sem=ag_send.at[step],
            recv_sem=ag_recv.at[step],
            device_id={"blk": source},
            device_id_type=MESH,
        ).wait_recv()

    for step in range(1, blocks):
        scatter(step).start()

    strips_arrive(meta, meta_send, meta_recv)
    reach_here = reach_ref[level].astype(F32) + 1.0
    lane_row = lax.broadcasted_iota(jnp.int32, (obs, rows), 1).astype(F32)
    columns = []
    for s in range(3):
        turned = jnp.transpose(
            jnp.concatenate([meta[s], jnp.zeros((LANES - 8, wide), F32)], axis=0)
        )
        columns.append([turned[:obs, i : i + 1] for i in range(3)])
    for s in range(3):
        col, row, lev = columns[s]
        vertical = jnp.maximum(0.0, 1.0 - jnp.abs(level.astype(F32) - lev) / reach_here)
        gap = lane_row - row
        gap = gap * gap
        for c in range(cols):
            across = col - (tile * cols + c).astype(F32)
            close = jnp.maximum(1.0 - (across * across + gap) * (1.0 / (cols * cols)), 0.0)
            taper_state[s, :, c * rows : (c + 1) * rows] = close * close * vertical

    for step in range(1, blocks):
        scatter(step).wait_recv()
    summed = picked[mine, :]
    for step in range(1, blocks):
        summed = summed + parts[step]
    near[0, 1, mine, :] = summed
    for step in range(1, blocks):
        gather(step).start()

    reach_own = jnp.zeros((1, wide), F32)
    for k in range(blocks):
        reach_own = jnp.where(own_level == float(k), reach_ref[k].astype(F32), reach_own)
    reach_own = 1.0 / (reach_own + 1.0)
    for s in range(3):
        col, row, lev = columns[s]
        across = col - own_col
        gap = row - own_row
        close = jnp.maximum(1.0 - (across * across + gap * gap) * (1.0 / (cols * cols)), 0.0)
        vertical = jnp.maximum(0.0, 1.0 - jnp.abs(own_level - lev) * reach_own)
        taper_obs[s] = close * close * vertical

    for step in range(1, blocks):
        gather_arrive(step)
    strips_start(near.at[0], halo_send.at[0], halo_recv.at[0])

    first_half = lax.broadcasted_iota(jnp.int32, (wide, LANES), 1) < members

    def statistics(turn):
        for s in range(3):
            prior = near[turn, s]
            average = jnp.sum(prior, axis=0, keepdims=True) * (1.0 / members)
            deviation = prior - average
            flag = meta[s, 4:5, :]
            error = jnp.where(flag > 0, meta[s, 6:7, :], 1.0)
            spread = jnp.sum(deviation * deviation, axis=0, keepdims=True) * (1.0 / (members - 1)) + error
            shrink = 1.0 / (1.0 + jnp.sqrt(error / spread))
            innovation = meta[s, 5:6, :] - average
            coefficient = jnp.where(flag == float(turn + 1), 1.0 / (spread * (members - 1)), 0.0)
            weighted = deviation * coefficient
            turned = jnp.transpose(jnp.concatenate([weighted, weighted], axis=0))
            high = turned.astype(BF16).astype(F32)
            both = jnp.where(first_half, high, turned - high).astype(BF16)[:obs]
            dev_t[s] = jnp.concatenate([both, both], axis=1)
            high, low = split(innovation - shrink * deviation)
            factor[s] = jnp.concatenate([high, low], axis=0)

    def update(x, taper):
        high, low = split(x)
        stacked = jnp.concatenate([high, high, low, low], axis=0)
        for s in range(3):
            gain = dot(dev_t[s], stacked) * taper(s)
            gain_high, gain_low = split(gain)
            both = dot(factor[s, :, :obs], gain_high)
            x = x + (both[:members] + both[members:] + dot(factor[s, :members, :obs], gain_low))
        return x

    for turn in range(NBATCH):
        strips_arrive(near.at[turn], halo_send.at[turn], halo_recv.at[turn])
        statistics(turn)
        if turn + 1 < NBATCH:
            near[turn + 1, 1] = update(near[turn, 1], lambda s: taper_obs[s])
            strips_start(near.at[turn + 1], halo_send.at[turn + 1], halo_recv.at[turn + 1])

        def field(f, carry, turn=turn):
            for half in range(cells // wide):
                at = slice(half * wide, (half + 1) * wide)
                per = wide // rows
                if turn == 0:
                    x = jnp.concatenate(
                        [
                            x_in[pl.ds(f * members * cols + half * per + c, members, stride=cols), :]
                            for c in range(per)
                        ],
                        axis=1,
                    )
                else:
                    x = state[f, :, at]
                x = update(x, lambda s: taper_state[s, :, at])
                if turn + 1 < NBATCH:
                    state[f, :, at] = x
                else:
                    for c in range(per):
                        out_ref[pl.ds(f * members * cols + half * per + c, members, stride=cols), :] = x[
                            :, c * rows : (c + 1) * rows
                        ]
            return carry

        lax.fori_loop(0, fields, field, 0)

    strips_sent(meta, meta_send, meta_recv)
    for step in range(1, blocks):
        scatter(step).wait_send()
        gather(step).wait_send()
    for turn in range(NBATCH):
        strips_sent(near.at[turn], halo_send.at[turn], halo_recv.at[turn])


def shards(
    tiles, blocks, ensemble, obs_col, obs_row, obs_level, obs_field, obs_batch, obs_value, obs_error, band_reach
):
    levels, fields, members, cols, rows = ensemble.shape
    obs = obs_col.shape[0]
    wide = 256
    cells = cols * rows
    sizes = (tiles, blocks, fields, members, cols, rows, obs, wide)
    any_space = pl.BlockSpec(memory_space=pltpu.HBM)
    vmem = pl.BlockSpec(memory_space=pltpu.VMEM)
    smem = pl.BlockSpec(memory_space=pltpu.SMEM)
    flat = fields * members * cols
    out = pl.pallas_call(
        functools.partial(kernel, sizes),
        out_shape=jax.ShapeDtypeStruct((flat, rows), F32),
        in_specs=[any_space] + [vmem] * 7 + [smem],
        out_specs=vmem,
        scratch_shapes=[
            pltpu.VMEM((flat, rows), F32),
            pltpu.VMEM((fields, members, cells), F32),
            pltpu.VMEM((NBATCH, 3, members, wide), F32),
            pltpu.VMEM((3, 8, wide), F32),
            pltpu.VMEM((3, obs, cells), F32),
            pltpu.VMEM((3, obs, wide), F32),
            pltpu.VMEM((members, wide), F32),
            pltpu.VMEM((blocks, members // blocks, wide), F32),
            pltpu.VMEM((3, obs, wide), BF16),
            pltpu.VMEM((3, 2 * members, wide), BF16),
            pltpu.SemaphoreType.DMA,
            pltpu.SemaphoreType.DMA((2,)),
            pltpu.SemaphoreType.DMA((2,)),
            pltpu.SemaphoreType.DMA((blocks,)),
            pltpu.SemaphoreType.DMA((blocks,)),
            pltpu.SemaphoreType.DMA((blocks,)),
            pltpu.SemaphoreType.DMA((blocks,)),
            pltpu.SemaphoreType.DMA((NBATCH, 2)),
            pltpu.SemaphoreType.DMA((NBATCH, 2)),
        ],
        compiler_params=pltpu.CompilerParams(
            collective_id=0, has_side_effects=True, vmem_limit_bytes=32 * 2**20
        ),
    )(
        ensemble.reshape(flat, rows),
        *(v.reshape(1, obs) for v in (obs_col, obs_row, obs_level, obs_field, obs_batch, obs_value, obs_error)),
        band_reach,
    )
    return out.reshape(levels, fields, members, cols, rows)


def solution(mesh):
    return jax.shard_map(
        functools.partial(shards, mesh.shape["tile"], mesh.shape["blk"]),
        mesh=mesh,
        in_specs=(
            P("blk", None, None, "tile", None),
            P("tile"),
            P("tile"),
            P("tile"),
            P("tile"),
            P("tile"),
            P("tile"),
            P("tile"),
            P(),
        ),
        out_specs=P("blk", None, None, "tile", None),
        check_vma=False,
    )
```

time: 223 us -> 45.2 us (0.20)
  the two profiles are of different devices: /device:TPU:256 before, /device:TPU:199 now
where the time goes in v1:
time: 45.2 us; the launch traced here: 45 us
  Pallas kernels  42.3 us (94%)
  local copies, waits for them, and re-layouts  2.66 us (6%)
    pallas_call x1, Pallas kernels, shards(): pl.pallas_call(functools.partial(kernel, sizes), out_shape=jax.ShapeDtype...  42.3 us
    unnamed x19, local copies, waits for them, and re-layouts  2.66 us

profile of v1, /device:TPU:199, one launch (start us, length us, event | category | flops | bytes accessed | tf_op | source)
XLA Modules:
  0.0 45.0 jit_solution(11549630163602341464)
XLA Ops:
  0.0 0.0 copy-start.6
  0.0 0.0 copy-start.7
  0.0 0.0 copy-start.4
  0.0 0.0 copy-start.5
  0.0 0.0 copy-start.2
  0.0 0.0 copy-start.3
  0.0 0.0 copy-start.1
  0.0 0.0 copy-start.8
  0.1 0.6 %copy-done.6 = f32[208]{0:T(256)S(1)} copy-done((f32[208]{0:T(256)S(1)}, f32[208]{0:T(256)}, u32[]{:S(2)}) %copy-start.6) | copy-done | bytes 856
  0.7 0.0 copy-done.7
  0.7 0.0 copy-done.4
  0.7 0.0 copy-done.5
  0.7 0.0 copy-done.2
  0.7 0.0 copy-done.3
  0.8 0.0 copy-done.1
  0.8 0.0 copy-done.8
  0.8 0.0 copy-start
  0.8 1.1 %copy-done = f32[1,5,64,4,128]{4,3,2,1,0:T(4,128)S(1)} copy-done((f32[1,5,64,4,128]{4,3,2,1,0:T(4,128)S(1)}, f32[1,5,64,4,128]{4,3,2,1,0:T(4,128)}, u32[]{:S(2)}) %copy-start) | copy-done | bytes 655384
  1.9 42.3 %shard_map.91 = f32[1280,128]{1,0:T(8,128)S(1)} custom-call(f32[1280,128]{1,0:T(8,128)S(1)} %bitcast.10, s32[1,208]{1,0:T(1,128)S(1)} %bitcast.11, s32[1,208]{1,0:T(1,128)S(1)} %bitcast.12, s32[1,208]{1,0:T(1,128)S(1)} %bitcast.13, s32[1,208]{1,0:T(1,128)S(1)} %bitcast.14, s32[1,208]{1,0:T(1,128)S(1)} %bitcast.15, f32[1,208]{1,0:T(1,128)S(1)} %bitcast.16, ...), custom_call_target="tpu_custom_call" | custom-call | tf_op jit(solution)/shard_map/pallas_call | solution.py:331
  44.2 0.8 %copy.11 = f32[1,5,64,4,128]{4,3,2,1,0:T(4,128)} copy(f32[1,5,64,4,128]{4,3,2,1,0:T(4,128)S(1)} %bitcast.9) | data formatting | bytes 1310720
Async XLA Ops:
  0.0 0.7 %copy-start.6 = (f32[208]{0:T(256)S(1)}, f32[208]{0:T(256)}, u32[]{:S(2)}) copy-start(f32[208]{0:T(256)} %param.15) | copy-start | bytes 2500
  0.0 0.7 %copy-start.7 = (f32[208]{0:T(256)S(1)}, f32[208]{0:T(256)}, u32[]{:S(2)}) copy-start(f32[208]{0:T(256)} %param.16) | copy-start | bytes 2500
  0.0 0.7 %copy-start.4 = (s32[208]{0:T(256)S(1)}, s32[208]{0:T(256)}, u32[]{:S(2)}) copy-start(s32[208]{0:T(256)} %param.13) | copy-start | bytes 2500
  0.0 0.7 %copy-start.5 = (s32[208]{0:T(256)S(1)}, s32[208]{0:T(256)}, u32[]{:S(2)}) copy-start(s32[208]{0:T(256)} %param.14) | copy-start | bytes 2500
  0.0 0.7 %copy-start.2 = (s32[208]{0:T(256)S(1)}, s32[208]{0:T(256)}, u32[]{:S(2)}) copy-start(s32[208]{0:T(256)} %param.11) | copy-start | bytes 2500
  0.0 0.7 %copy-start.3 = (s32[208]{0:T(256)S(1)}, s32[208]{0:T(256)}, u32[]{:S(2)}) copy-start(s32[208]{0:T(256)} %param.12) | copy-start | bytes 2500
  0.0 0.7 %copy-start.1 = (s32[208]{0:T(256)S(1)}, s32[208]{0:T(256)}, u32[]{:S(2)}) copy-start(s32[208]{0:T(256)} %param.10) | copy-start | bytes 2500
  0.0 0.7 %copy-start.8 = (s32[8]{0:T(128)S(1)}, s32[8]{0:T(128)}, u32[]{:S(2)}) copy-start(s32[8]{0:T(128)} %reach_ref.1) | copy-start | bytes 100
  0.8 1.1 %copy-start = (f32[1,5,64,4,128]{4,3,2,1,0:T(4,128)S(1)}, f32[1,5,64,4,128]{4,3,2,1,0:T(4,128)}, u32[]{:S(2)}) copy-start(f32[1,5,64,4,128]{4,3,2,1,0:T(4,128)} %param.9) | copy-start | bytes 1966084

commit v2 on v1

--- a/solution.py
+++ b/solution.py
@@ -12,6 +12,7 @@
 F32 = jnp.float32
 BF16 = jnp.bfloat16
 LANES = 128
+VMEM_LIMIT = 62
 
 
 def split(x):
@@ -46,6 +47,9 @@
     parts,
     dev_t,
     factor,
+    places,
+    values,
+    place_sem,
     load_sem,
     meta_send,
     meta_recv,
@@ -57,15 +61,13 @@
     halo_recv,
 ):
     tiles, blocks, fields, members, cols, rows, obs, wide = sizes
+    near_obs = dev_t.shape[0]
     cells = cols * rows
     share = members // blocks
     tile = lax.axis_index("tile")
     level = lax.axis_index("blk")
     has_left, has_right = tile > 0, tile < tiles - 1
 
-    load = pltpu.make_async_copy(x_hbm, x_in, load_sem)
-    load.start()
-
     barrier = pltpu.get_barrier_semaphore()
     for step in range(1, blocks):
         pl.semaphore_signal(
@@ -80,14 +82,25 @@
     def _():
         pl.semaphore_signal(barrier, inc=1, device_id={"tile": tile + 1}, device_id_type=MESH)
 
-    meta[1] = jnp.zeros((8, wide), F32)
-    meta[1, 0:1, :obs] = col_ref[...].astype(F32)
-    meta[1, 1:2, :obs] = row_ref[...].astype(F32)
-    meta[1, 2:3, :obs] = level_ref[...].astype(F32)
-    meta[1, 3:4, :obs] = field_ref[...].astype(F32)
-    meta[1, 4:5, :obs] = (batch_ref[...] + 1).astype(F32)
-    meta[1, 5:6, :obs] = value_ref[...]
-    meta[1, 6:7, :obs] = error_ref[...]
+    brought = [
+        pltpu.make_async_copy(ref, places.at[i], place_sem.at[i])
+        for i, ref in enumerate((col_ref, row_ref, level_ref, field_ref, batch_ref))
+    ] + [
+        pltpu.make_async_copy(ref, values.at[i], place_sem.at[5 + i])
+        for i, ref in enumerate((value_ref, error_ref))
+    ]
+    for copy in brought:
+        copy.start()
+    loads = [
+        pltpu.make_async_copy(
+            x_hbm.at[pl.ds(f * members * cols, members * cols)],
+            x_in.at[pl.ds(f * members * cols, members * cols)],
+            load_sem.at[f],
+        )
+        for f in range(fields)
+    ]
+    for copy in loads:
+        copy.start()
 
     @pl.when(jnp.logical_not(has_left))
     def _():
@@ -99,9 +112,13 @@
         near[:, 2] = jnp.zeros((NBATCH, members, wide), F32)
         meta[2] = jnp.zeros((8, wide), F32)
 
-    pl.semaphore_wait(
-        barrier, (blocks - 1) + has_left.astype(jnp.int32) + has_right.astype(jnp.int32)
-    )
+    meta[1] = jnp.zeros((8, wide), F32)
+    for copy in brought:
+        copy.wait()
+    for i in range(5):
+        meta[1, i : i + 1, :obs] = (places[i] + (1 if i == 4 else 0)).astype(F32)
+    for i in range(2):
+        meta[1, 5 + i : 6 + i, :obs] = values[i]
 
     def strips(array, send, recv):
         right = pltpu.make_async_remote_copy(
@@ -137,13 +154,10 @@
         pl.when(has_right)(right.wait_send)
         pl.when(has_left)(left.wait_send)
 
-    strips_start(meta, meta_send, meta_recv)
-
     own_col, own_row, own_level, own_field = (meta[1, i : i + 1, :] for i in range(4))
     here = (own_level == level.astype(F32)) & (meta[1, 4:5, :] > 0)
     place = (own_field * cols + own_col - (tile * cols).astype(F32)) * rows + own_row
     place = jnp.where(here, place, -1.0)
-    load.wait()
     cell_at = lax.broadcasted_iota(jnp.int32, (cells, wide), 0).astype(F32)
 
     def slab(ref, f):
@@ -153,6 +167,7 @@
 
     total = jnp.zeros((3 * members, wide), F32)
     for f in range(fields):
+        loads[f].wait()
         x = slab(x_in, f)
         high = x.astype(BF16)
         rest = x - high.astype(F32)
@@ -197,11 +212,18 @@
             device_id_type=MESH,
         ).wait_recv()
 
+    pl.semaphore_wait(
+        barrier, (blocks - 1) + has_left.astype(jnp.int32) + has_right.astype(jnp.int32)
+    )
     for step in range(1, blocks):
         scatter(step).start()
+    strips_start(meta, meta_send, meta_recv)
 
     strips_arrive(meta, meta_send, meta_recv)
     reach_here = reach_ref[level].astype(F32) + 1.0
+    taper_state[3 * obs :] = jnp.zeros((near_obs - 3 * obs, cells), F32)
+    taper_obs[3 * obs :] = jnp.zeros((near_obs - 3 * obs, wide), F32)
+    dev_t[3 * obs :] = jnp.zeros((near_obs - 3 * obs, wide), BF16)
     lane_row = lax.broadcasted_iota(jnp.int32, (obs, rows), 1).astype(F32)
     columns = []
     for s in range(3):
@@ -217,7 +239,7 @@
         for c in range(cols):
             across = col - (tile * cols + c).astype(F32)
             close = jnp.maximum(1.0 - (across * across + gap) * (1.0 / (cols * cols)), 0.0)
-            taper_state[s, :, c * rows : (c + 1) * rows] = close * close * vertical
+            taper_state[s * obs : (s + 1) * obs, c * rows : (c + 1) * rows] = close * close * vertical
 
     for step in range(1, blocks):
         scatter(step).wait_recv()
@@ -238,7 +260,7 @@
         gap = row - own_row
         close = jnp.maximum(1.0 - (across * across + gap * gap) * (1.0 / (cols * cols)), 0.0)
         vertical = jnp.maximum(0.0, 1.0 - jnp.abs(own_level - lev) * reach_own)
-        taper_obs[s] = close * close * vertical
+        taper_obs[s * obs : (s + 1) * obs] = close * close * vertical
 
     for step in range(1, blocks):
         gather_arrive(step)
@@ -247,6 +269,7 @@
     first_half = lax.broadcasted_iota(jnp.int32, (wide, LANES), 1) < members
 
     def statistics(turn):
+        pulls = []
         for s in range(3):
             prior = near[turn, s]
             average = jnp.sum(prior, axis=0, keepdims=True) * (1.0 / members)
@@ -261,49 +284,37 @@
             turned = jnp.transpose(jnp.concatenate([weighted, weighted], axis=0))
             high = turned.astype(BF16).astype(F32)
             both = jnp.where(first_half, high, turned - high).astype(BF16)[:obs]
-            dev_t[s] = jnp.concatenate([both, both], axis=1)
-            high, low = split(innovation - shrink * deviation)
-            factor[s] = jnp.concatenate([high, low], axis=0)
+            dev_t[s * obs : (s + 1) * obs] = jnp.concatenate([both, both], axis=1)
+            pulls.append((innovation - shrink * deviation)[:, :obs])
+        pulls.append(jnp.zeros((members, near_obs - 3 * obs), F32))
+        high, low = split(jnp.concatenate(pulls, axis=1))
+        factor[...] = jnp.concatenate([high, low], axis=0)
 
     def update(x, taper):
         high, low = split(x)
         stacked = jnp.concatenate([high, high, low, low], axis=0)
-        for s in range(3):
-            gain = dot(dev_t[s], stacked) * taper(s)
-            gain_high, gain_low = split(gain)
-            both = dot(factor[s, :, :obs], gain_high)
-            x = x + (both[:members] + both[members:] + dot(factor[s, :members, :obs], gain_low))
+        gain_high, gain_low = split(dot(dev_t[...], stacked) * taper())
+        both = dot(factor[...], gain_high)
+        x = x + (both[:members] + both[members:] + dot(factor[:members], gain_low))
         return x
 
     for turn in range(NBATCH):
         strips_arrive(near.at[turn], halo_send.at[turn], halo_recv.at[turn])
         statistics(turn)
         if turn + 1 < NBATCH:
-            near[turn + 1, 1] = update(near[turn, 1], lambda s: taper_obs[s])
+            near[turn + 1, 1] = update(near[turn, 1], lambda: taper_obs[...])
             strips_start(near.at[turn + 1], halo_send.at[turn + 1], halo_recv.at[turn + 1])
 
         def field(f, carry, turn=turn):
-            for half in range(cells // wide):
-                at = slice(half * wide, (half + 1) * wide)
-                per = wide // rows
-                if turn == 0:
-                    x = jnp.concatenate(
-                        [
-                            x_in[pl.ds(f * members * cols + half * per + c, members, stride=cols), :]
-                            for c in range(per)
-                        ],
-                        axis=1,
-                    )
-                else:
-                    x = state[f, :, at]
-                x = update(x, lambda s: taper_state[s, :, at])
-                if turn + 1 < NBATCH:
-                    state[f, :, at] = x
-                else:
-                    for c in range(per):
-                        out_ref[pl.ds(f * members * cols + half * per + c, members, stride=cols), :] = x[
-                            :, c * rows : (c + 1) * rows
-                        ]
+            x = slab(x_in, f) if turn == 0 else state[f]
+            x = update(x, lambda: taper_state[...])
+            if turn + 1 < NBATCH:
+                state[f] = x
+            else:
+                for c in range(cols):
+                    out_ref[pl.ds(f * members * cols + c, members, stride=cols), :] = x[
+                        :, c * rows : (c + 1) * rows
+                    ]
             return carry
 
         lax.fori_loop(0, fields, field, 0)
@@ -328,23 +339,27 @@
     vmem = pl.BlockSpec(memory_space=pltpu.VMEM)
     smem = pl.BlockSpec(memory_space=pltpu.SMEM)
     flat = fields * members * cols
+    near_obs = -(-3 * obs // 32) * 32
     out = pl.pallas_call(
         functools.partial(kernel, sizes),
         out_shape=jax.ShapeDtypeStruct((flat, rows), F32),
-        in_specs=[any_space] + [vmem] * 7 + [smem],
+        in_specs=[any_space] * 8 + [smem],
         out_specs=vmem,
         scratch_shapes=[
             pltpu.VMEM((flat, rows), F32),
             pltpu.VMEM((fields, members, cells), F32),
             pltpu.VMEM((NBATCH, 3, members, wide), F32),
             pltpu.VMEM((3, 8, wide), F32),
-            pltpu.VMEM((3, obs, cells), F32),
-            pltpu.VMEM((3, obs, wide), F32),
+            pltpu.VMEM((near_obs, cells), F32),
+            pltpu.VMEM((near_obs, wide), F32),
             pltpu.VMEM((members, wide), F32),
             pltpu.VMEM((blocks, members // blocks, wide), F32),
-            pltpu.VMEM((3, obs, wide), BF16),
-            pltpu.VMEM((3, 2 * members, wide), BF16),
-            pltpu.SemaphoreType.DMA,
+            pltpu.VMEM((near_obs, wide), BF16),
+            pltpu.VMEM((2 * members, near_obs), BF16),
+            pltpu.VMEM((5, 1, obs), jnp.int32),
+            pltpu.VMEM((2, 1, obs), F32),
+            pltpu.SemaphoreType.DMA((7,)),
+            pltpu.SemaphoreType.DMA((fields,)),
             pltpu.SemaphoreType.DMA((2,)),
             pltpu.SemaphoreType.DMA((2,)),
             pltpu.SemaphoreType.DMA((blocks,)),
@@ -355,7 +370,7 @@
             pltpu.SemaphoreType.DMA((NBATCH, 2)),
         ],
         compiler_params=pltpu.CompilerParams(
-            collective_id=0, has_side_effects=True, vmem_limit_bytes=32 * 2**20
+            collective_id=0, has_side_effects=True, vmem_limit_bytes=VMEM_LIMIT * 2**20
         ),
     )(
         ensemble.reshape(flat, rows),

time: 45.2 us -> 44.2 us (0.978)
  the two profiles are of different devices: /device:TPU:199 before, /device:TPU:256 now
where the time goes in v2:
time: 44.2 us; the launch traced here: 44 us
  Pallas kernels  42 us (95%)
  local copies, waits for them, and re-layouts  1.97 us (4%)
    pallas_call x1, Pallas kernels, shards(): pl.pallas_call(functools.partial(kernel, sizes), out_shape=jax.ShapeDtype...  42 us
    unnamed x1, local copies, waits for them, and re-layouts  1.97 us

profile of v2, /device:TPU:256, one launch (start us, length us, event | category | flops | bytes accessed | tf_op | source)
XLA Modules:
  0.0 44.0 jit_solution(12458124015603976793)
XLA Ops:
  0.0 42.0 %shard_map.91 = f32[1280,128]{1,0:T(8,128)} custom-call(f32[1280,128]{1,0:T(8,128)} %bitcast.10, s32[1,208]{1,0:T(1,128)} %bitcast.11, s32[1,208]{1,0:T(1,128)} %bitcast.12, s32[1,208]{1,0:T(1,128)} %bitcast.13, s32[1,208]{1,0:T(1,128)} %bitcast.14, s32[1,208]{1,0:T(1,128)} %bitcast.15, f32[1,208]{1,0:T(1,128)} %bitcast.16, f32[1,208]{1,0:T(1,128)} %bitcast.17, ...), custom_call_target="tpu_custom_call" | custom-call | tf_op jit(solution)/shard_map/pallas_call | solution.py:343
  42.0 2.0 %copy.11 = f32[1,5,64,4,128]{4,3,2,1,0:T(4,128)} copy(f32[1,5,64,4,128]{4,3,2,1,0:T(4,128)} %bitcast.9) | data formatting | bytes 1310720

commit v3 on v2

--- a/solution.py
+++ b/solution.py
@@ -12,7 +12,7 @@
 F32 = jnp.float32
 BF16 = jnp.bfloat16
 LANES = 128
-VMEM_LIMIT = 62
+VMEM_LIMIT = 24
 
 
 def split(x):
@@ -23,6 +23,42 @@
 
 def dot(a, b):
     return jnp.dot(a, b, preferred_element_type=F32)
+
+
+def update(x, dev_t, factor, taper):
+    members = x.shape[0]
+    high, low = split(x)
+    stacked = jnp.concatenate([high, high, low, low], axis=0)
+    gain_high, gain_low = split(dot(dev_t[...], stacked) * taper)
+    both = dot(factor[...], gain_high)
+    return x + (both[:members] + both[members:] + dot(factor[:members], gain_low))
+
+
+def update_fields(xs, dev_t, factor, taper_state):
+    taper = jnp.concatenate([taper_state[...]] * len(xs), axis=1)
+    x = update(jnp.concatenate(xs, axis=1), dev_t, factor, taper)
+    cells = x.shape[1] // len(xs)
+    return [x[:, i * cells : (i + 1) * cells] for i in range(len(xs))]
+
+
+def groups(fields):
+    return [list(range(f, min(f + 2, fields))) for f in range(0, fields, 2)]
+
+
+def finish(sizes, state, dev_t, factor, taper_state, out_hbm, out, out_sem):
+    fields, members, cols, rows = sizes
+    flat = members * cols
+    copies = []
+    for group in groups(fields):
+        done = update_fields([state[f] for f in group], dev_t, factor, taper_state)
+        for f, x in zip(group, done):
+            for c in range(cols):
+                out[pl.ds(f * flat + c, members, stride=cols), :] = x[:, c * rows : (c + 1) * rows]
+            part = pl.ds(f * flat, flat)
+            copies.append(pltpu.make_async_copy(out.at[part], out_hbm.at[part], out_sem.at[f]))
+            copies[-1].start()
+    for copy in copies:
+        copy.wait()
 
 
 def kernel(
@@ -35,20 +71,21 @@
     batch_ref,
     value_ref,
     error_ref,
-    reach_ref,
-    out_ref,
+    reach_hbm,
+    state,
+    dev_t,
+    factor,
+    taper_state,
     x_in,
-    state,
     near,
     meta,
-    taper_state,
     taper_obs,
     picked,
     parts,
-    dev_t,
-    factor,
     places,
     values,
+    reach_ref,
+    reach_sem,
     place_sem,
     load_sem,
     meta_send,
@@ -89,6 +126,8 @@
         pltpu.make_async_copy(ref, values.at[i], place_sem.at[5 + i])
         for i, ref in enumerate((value_ref, error_ref))
     ]
+    reach_copy = pltpu.make_async_copy(reach_hbm, reach_ref, reach_sem)
+    reach_copy.start()
     for copy in brought:
         copy.start()
     loads = [
@@ -220,6 +259,7 @@
     strips_start(meta, meta_send, meta_recv)
 
     strips_arrive(meta, meta_send, meta_recv)
+    reach_copy.wait()
     reach_here = reach_ref[level].astype(F32) + 1.0
     taper_state[3 * obs :] = jnp.zeros((near_obs - 3 * obs, cells), F32)
     taper_obs[3 * obs :] = jnp.zeros((near_obs - 3 * obs, wide), F32)
@@ -290,34 +330,16 @@
         high, low = split(jnp.concatenate(pulls, axis=1))
         factor[...] = jnp.concatenate([high, low], axis=0)
 
-    def update(x, taper):
-        high, low = split(x)
-        stacked = jnp.concatenate([high, high, low, low], axis=0)
-        gain_high, gain_low = split(dot(dev_t[...], stacked) * taper())
-        both = dot(factor[...], gain_high)
-        x = x + (both[:members] + both[members:] + dot(factor[:members], gain_low))
-        return x
-
     for turn in range(NBATCH):
         strips_arrive(near.at[turn], halo_send.at[turn], halo_recv.at[turn])
         statistics(turn)
         if turn + 1 < NBATCH:
-            near[turn + 1, 1] = update(near[turn, 1], lambda: taper_obs[...])
+            near[turn + 1, 1] = update(near[turn, 1], dev_t, factor, taper_obs[...])
             strips_start(near.at[turn + 1], halo_send.at[turn + 1], halo_recv.at[turn + 1])
-
-        def field(f, carry, turn=turn):
-            x = slab(x_in, f) if turn == 0 else state[f]
-            x = update(x, lambda: taper_state[...])
-            if turn + 1 < NBATCH:
-                state[f] = x
-            else:
-                for c in range(cols):
-                    out_ref[pl.ds(f * members * cols + c, members, stride=cols), :] = x[
-                        :, c * rows : (c + 1) * rows
-                    ]
-            return carry
-
-        lax.fori_loop(0, fields, field, 0)
+            for group in groups(fields):
+                xs = [slab(x_in, f) if turn == 0 else state[f] for f in group]
+                for f, x in zip(group, update_fields(xs, dev_t, factor, taper_state)):
+                    state[f] = x
 
     strips_sent(meta, meta_send, meta_recv)
     for step in range(1, blocks):
@@ -337,27 +359,30 @@
     sizes = (tiles, blocks, fields, members, cols, rows, obs, wide)
     any_space = pl.BlockSpec(memory_space=pltpu.HBM)
     vmem = pl.BlockSpec(memory_space=pltpu.VMEM)
-    smem = pl.BlockSpec(memory_space=pltpu.SMEM)
+    in_hbm = functools.partial(pltpu.with_memory_space_constraint, memory_space=pltpu.HBM)
     flat = fields * members * cols
     near_obs = -(-3 * obs // 32) * 32
-    out = pl.pallas_call(
+    made = pl.pallas_call(
         functools.partial(kernel, sizes),
-        out_shape=jax.ShapeDtypeStruct((flat, rows), F32),
-        in_specs=[any_space] * 8 + [smem],
-        out_specs=vmem,
+        out_shape=(
+            jax.ShapeDtypeStruct((fields, members, cells), F32),
+            jax.ShapeDtypeStruct((near_obs, wide), BF16),
+            jax.ShapeDtypeStruct((2 * members, near_obs), BF16),
+            jax.ShapeDtypeStruct((near_obs, cells), F32),
+        ),
+        in_specs=[any_space] * 9,
+        out_specs=[vmem] * 4,
         scratch_shapes=[
             pltpu.VMEM((flat, rows), F32),
-            pltpu.VMEM((fields, members, cells), F32),
             pltpu.VMEM((NBATCH, 3, members, wide), F32),
             pltpu.VMEM((3, 8, wide), F32),
-            pltpu.VMEM((near_obs, cells), F32),
             pltpu.VMEM((near_obs, wide), F32),
             pltpu.VMEM((members, wide), F32),
             pltpu.VMEM((blocks, members // blocks, wide), F32),
-            pltpu.VMEM((near_obs, wide), BF16),
-            pltpu.VMEM((2 * members, near_obs), BF16),
             pltpu.VMEM((5, 1, obs), jnp.int32),
             pltpu.VMEM((2, 1, obs), F32),
+            pltpu.SMEM((blocks,), jnp.int32),
+            pltpu.SemaphoreType.DMA,
             pltpu.SemaphoreType.DMA((7,)),
             pltpu.SemaphoreType.DMA((fields,)),
             pltpu.SemaphoreType.DMA((2,)),
@@ -373,10 +398,21 @@
             collective_id=0, has_side_effects=True, vmem_limit_bytes=VMEM_LIMIT * 2**20
         ),
     )(
-        ensemble.reshape(flat, rows),
-        *(v.reshape(1, obs) for v in (obs_col, obs_row, obs_level, obs_field, obs_batch, obs_value, obs_error)),
-        band_reach,
+        in_hbm(ensemble.reshape(flat, rows)),
+        *(
+            in_hbm(v.reshape(1, obs))
+            for v in (obs_col, obs_row, obs_level, obs_field, obs_batch, obs_value, obs_error)
+        ),
+        in_hbm(band_reach),
     )
+    out = pl.pallas_call(
+        functools.partial(finish, (fields, members, cols, rows)),
+        out_shape=jax.ShapeDtypeStruct((flat, rows), F32),
+        in_specs=[vmem] * 4,
+        out_specs=any_space,
+        scratch_shapes=[pltpu.VMEM((flat, rows), F32), pltpu.SemaphoreType.DMA((fields,))],
+        compiler_params=pltpu.CompilerParams(vmem_limit_bytes=VMEM_LIMIT * 2**20),
+    )(*made)
     return out.reshape(levels, fields, members, cols, rows)
 
 

time: 44.2 us -> 40.4 us (0.914)
  local copies, waits for them, and re-layouts: 1.97 us -> 0 us
  Pallas kernels: 42 us -> 40.2 us
    unnamed x1 -> x0, local copies, waits for them, and re-layouts: 1.97 us -> none
    pallas_call x1 -> x2, Pallas kernels: 42 us -> 40.2 us  [the longest x1 37.4 us: shards(): pl.pallas_call(functools.partial(kernel, sizes), out_shape=(jax.ShapeDtyp...]
where the time goes in v3:
time: 40.4 us; the launch traced here: 40.2 us
  Pallas kernels  40.2 us (100%)
    pallas_call x1, Pallas kernels, shards(): pl.pallas_call(functools.partial(kernel, sizes), out_shape=(jax.ShapeDtyp...  37.4 us
    pallas_call x1, Pallas kernels, shards(): pl.pallas_call(functools.partial(finish, (fields, members, cols, rows)),...  2.88 us

profile of v3, /device:TPU:256, one launch (start us, length us, event | category | flops | bytes accessed | tf_op | source)
XLA Modules:
  0.0 40.2 jit_solution(12221755535608411516)
XLA Ops:
  0.0 37.4 %shard_map.91 = (f32[5,64,512]{2,1,0:T(8,128)S(1)}, bf16[640,256]{1,0:T(8,128)(2,1)S(1)}, bf16[128,640]{1,0:T(8,128)(2,1)S(1)}, f32[640,512]{1,0:T(8,128)S(1)}) custom-call(f32[1280,128]{1,0:T(8,128)} %bitcast.9, s32[1,208]{1,0:T(1,128)} %bitcast.10, s32[1,208]{1,0:T(1,128)} %bitcast.11, s32[1,208]{1,0:T(1,128)} %bitcast.12, s32[1,208]{1,0:T(1,128)} %bitcast.13, ...), custom_call_target="tpu_custom_call" | custom-call | tf_op jit(solution)/shard_map/pallas_call | solution.py:365
  37.4 2.9 %shard_map.92 = f32[1280,128]{1,0:T(8,128)} custom-call(f32[5,64,512]{2,1,0:T(8,128)S(1)} %get-tuple-element.9.state, bf16[640,256]{1,0:T(8,128)(2,1)S(1)} %get-tuple-element.10.dev_t, bf16[128,640]{1,0:T(8,128)(2,1)S(1)} %get-tuple-element.11.factor, f32[640,512]{1,0:T(8,128)S(1)} %get-tuple-element.12.taper_state), custom_call_target="tpu_custom_call" | custom-call | tf_op jit(solution)/shard_map/pallas_call | solution.py:408

commit v4 on v3

--- a/solution.py
+++ b/solution.py
@@ -13,6 +13,7 @@
 BF16 = jnp.bfloat16
 LANES = 128
 VMEM_LIMIT = 24
+SHORT = 80
 
 
 def split(x):
@@ -21,8 +22,21 @@
     return high, low
 
 
+def sort_key(flag, axis):
+    turn = jnp.where(flag > 0, NBATCH - flag, float(NBATCH))
+    at = lax.broadcasted_iota(jnp.int32, flag.shape, axis).astype(F32)
+    return turn * float(flag.shape[axis]) + at
+
+
 def dot(a, b):
     return jnp.dot(a, b, preferred_element_type=F32)
+
+
+def side_by_side(pulls, width):
+    have = sum(pull.shape[1] for pull in pulls)
+    pulls = pulls + [jnp.zeros((pulls[0].shape[0], width - have), F32)]
+    high, low = split(jnp.concatenate(pulls, axis=1))
+    return jnp.concatenate([high, low], axis=0)
 
 
 def update(x, dev_t, factor, taper):
@@ -34,8 +48,8 @@
     return x + (both[:members] + both[members:] + dot(factor[:members], gain_low))
 
 
-def update_fields(xs, dev_t, factor, taper_state):
-    taper = jnp.concatenate([taper_state[...]] * len(xs), axis=1)
+def update_fields(xs, dev_t, factor, taper):
+    taper = jnp.concatenate([taper] * len(xs), axis=1)
     x = update(jnp.concatenate(xs, axis=1), dev_t, factor, taper)
     cells = x.shape[1] // len(xs)
     return [x[:, i * cells : (i + 1) * cells] for i in range(len(xs))]
@@ -45,20 +59,37 @@
     return [list(range(f, min(f + 2, fields))) for f in range(0, fields, 2)]
 
 
-def finish(sizes, state, dev_t, factor, taper_state, out_hbm, out, out_sem):
-    fields, members, cols, rows = sizes
+def finish(sizes, state, dev_t, factor, taper_state, short_factor, most, out_hbm, out, out_sem):
+    fields, members, cols, rows, obs = sizes
     flat = members * cols
-    copies = []
-    for group in groups(fields):
-        done = update_fields([state[f] for f in group], dev_t, factor, taper_state)
-        for f, x in zip(group, done):
-            for c in range(cols):
-                out[pl.ds(f * flat + c, members, stride=cols), :] = x[:, c * rows : (c + 1) * rows]
-            part = pl.ds(f * flat, flat)
-            copies.append(pltpu.make_async_copy(out.at[part], out_hbm.at[part], out_sem.at[f]))
-            copies[-1].start()
-    for copy in copies:
-        copy.wait()
+
+    def run(dev, pull, taper):
+        copies = []
+        for group in groups(fields):
+            done = update_fields([state[f] for f in group], dev, pull, taper)
+            for f, x in zip(group, done):
+                for c in range(cols):
+                    out[pl.ds(f * flat + c, members, stride=cols), :] = x[:, c * rows : (c + 1) * rows]
+                part = pl.ds(f * flat, flat)
+                copies.append(pltpu.make_async_copy(out.at[part], out_hbm.at[part], out_sem.at[f]))
+                copies[-1].start()
+        for copy in copies:
+            copy.wait()
+
+    few = jnp.max(most[...]) <= float(SHORT)
+
+    @pl.when(few)
+    def _():
+        def starts(array):
+            pieces = [array[s * obs : s * obs + SHORT] for s in range(3)]
+            rest = short_factor.shape[1] - 3 * SHORT
+            return jnp.concatenate(pieces + [jnp.zeros((rest, array.shape[1]), array.dtype)], axis=0)
+
+        run(starts(dev_t), short_factor, starts(taper_state))
+
+    @pl.when(jnp.logical_not(few))
+    def _():
+        run(dev_t, factor, taper_state[...])
 
 
 def kernel(
@@ -76,12 +107,15 @@
     dev_t,
     factor,
     taper_state,
+    short_factor,
+    most,
     x_in,
     near,
     meta,
     taper_obs,
     picked,
     parts,
+    drawn,
     places,
     values,
     reach_ref,
@@ -96,6 +130,8 @@
     ag_recv,
     halo_send,
     halo_recv,
+    piece_send,
+    piece_recv,
 ):
     tiles, blocks, fields, members, cols, rows, obs, wide = sizes
     near_obs = dev_t.shape[0]
@@ -106,7 +142,7 @@
     has_left, has_right = tile > 0, tile < tiles - 1
 
     barrier = pltpu.get_barrier_semaphore()
-    for step in range(1, blocks):
+    for step in (4, 3, 5, 2, 6, 1, 7):
         pl.semaphore_signal(
             barrier, inc=1, device_id={"blk": lax.rem(level + step, blocks)}, device_id_type=MESH
         )
@@ -151,13 +187,25 @@
         near[:, 2] = jnp.zeros((NBATCH, members, wide), F32)
         meta[2] = jnp.zeros((8, wide), F32)
 
-    meta[1] = jnp.zeros((8, wide), F32)
+    drawn[...] = jnp.zeros_like(drawn)
     for copy in brought:
         copy.wait()
     for i in range(5):
-        meta[1, i : i + 1, :obs] = (places[i] + (1 if i == 4 else 0)).astype(F32)
+        drawn[i : i + 1, :obs] = (places[i] + (1 if i == 4 else 0)).astype(F32)
     for i in range(2):
-        meta[1, 5 + i : 6 + i, :obs] = values[i]
+        drawn[5 + i : 6 + i, :obs] = values[i]
+    unsorted = drawn[...]
+    key = sort_key(unsorted[4:5], 1)
+    turned = jnp.transpose(jnp.concatenate([unsorted, jnp.zeros((LANES - 8, wide), F32)], axis=0))
+    key_column = sort_key(turned[:, 4:5], 0)
+    rank = jnp.sum(jnp.where(key < key_column, 1.0, 0.0), axis=1, keepdims=True)
+    moved = jnp.where(rank == lax.broadcasted_iota(jnp.int32, (wide, wide), 1).astype(F32), 1.0, 0.0)
+    high = unsorted.astype(BF16).astype(F32)
+    middle = (unsorted - high).astype(BF16).astype(F32)
+    low = unsorted - high - middle
+    terms = jnp.concatenate([high, middle, low, jnp.zeros_like(low)], axis=0).astype(BF16)
+    terms = dot(terms, moved.astype(BF16))
+    meta[1] = terms[:8] + terms[8:16] + terms[16:24]
 
     def strips(array, send, recv):
         right = pltpu.make_async_remote_copy(
@@ -254,7 +302,7 @@
     pl.semaphore_wait(
         barrier, (blocks - 1) + has_left.astype(jnp.int32) + has_right.astype(jnp.int32)
     )
-    for step in range(1, blocks):
+    for step in (4, 3, 5, 2, 6, 1, 7):
         scatter(step).start()
     strips_start(meta, meta_send, meta_recv)
 
@@ -287,8 +335,35 @@
     for step in range(1, blocks):
         summed = summed + parts[step]
     near[0, 1, mine, :] = summed
-    for step in range(1, blocks):
+    for step in (4, 3, 5, 2, 6, 1, 7):
         gather(step).start()
+
+    def pieces(source):
+        at = pl.ds(pl.multiple_of(source * share, share), share)
+        right = pltpu.make_async_remote_copy(
+            src_ref=near.at[0, 1, at],
+            dst_ref=near.at[0, 0, at],
+            send_sem=piece_send.at[0, source],
+            recv_sem=piece_recv.at[0, source],
+            device_id={"tile": jnp.minimum(tile + 1, tiles - 1)},
+            device_id_type=MESH,
+        )
+        left = pltpu.make_async_remote_copy(
+            src_ref=near.at[0, 1, at],
+            dst_ref=near.at[0, 2, at],
+            send_sem=piece_send.at[1, source],
+            recv_sem=piece_recv.at[1, source],
+            device_id={"tile": jnp.maximum(tile - 1, 0)},
+            device_id_type=MESH,
+        )
+        return right, left
+
+    def piece_start(source):
+        right, left = pieces(source)
+        pl.when(has_right)(right.start)
+        pl.when(has_left)(left.start)
+
+    piece_start(level)
 
     reach_own = jnp.zeros((1, wide), F32)
     for k in range(blocks):
@@ -302,9 +377,9 @@
         vertical = jnp.maximum(0.0, 1.0 - jnp.abs(own_level - lev) * reach_own)
         taper_obs[s * obs : (s + 1) * obs] = close * close * vertical
 
-    for step in range(1, blocks):
+    for step in (1, 7, 2, 6, 3, 5, 4):
         gather_arrive(step)
-    strips_start(near.at[0], halo_send.at[0], halo_recv.at[0])
+        piece_start(lax.rem(level + blocks - step, blocks))
 
     first_half = lax.broadcasted_iota(jnp.int32, (wide, LANES), 1) < members
 
@@ -326,26 +401,41 @@
             both = jnp.where(first_half, high, turned - high).astype(BF16)[:obs]
             dev_t[s * obs : (s + 1) * obs] = jnp.concatenate([both, both], axis=1)
             pulls.append((innovation - shrink * deviation)[:, :obs])
-        pulls.append(jnp.zeros((members, near_obs - 3 * obs), F32))
-        high, low = split(jnp.concatenate(pulls, axis=1))
-        factor[...] = jnp.concatenate([high, low], axis=0)
+        factor[...] = side_by_side(pulls, near_obs)
+        if turn + 1 == NBATCH:
+            short_factor[...] = side_by_side([pull[:, :SHORT] for pull in pulls], wide)
+            counts = [
+                jnp.sum(jnp.where(meta[s, 4:5, :] == float(NBATCH), 1.0, 0.0), axis=1, keepdims=True)
+                for s in range(3)
+            ]
+            most[...] = jnp.broadcast_to(functools.reduce(jnp.maximum, counts), (8, LANES))
 
     for turn in range(NBATCH):
-        strips_arrive(near.at[turn], halo_send.at[turn], halo_recv.at[turn])
+        if turn:
+            strips_arrive(near.at[turn], halo_send.at[turn], halo_recv.at[turn])
+        else:
+            for source in range(blocks):
+                right, left = pieces(source)
+                pl.when(has_left)(right.wait_recv)
+                pl.when(has_right)(left.wait_recv)
         statistics(turn)
         if turn + 1 < NBATCH:
             near[turn + 1, 1] = update(near[turn, 1], dev_t, factor, taper_obs[...])
             strips_start(near.at[turn + 1], halo_send.at[turn + 1], halo_recv.at[turn + 1])
             for group in groups(fields):
                 xs = [slab(x_in, f) if turn == 0 else state[f] for f in group]
-                for f, x in zip(group, update_fields(xs, dev_t, factor, taper_state)):
+                for f, x in zip(group, update_fields(xs, dev_t, factor, taper_state[...])):
                     state[f] = x
 
     strips_sent(meta, meta_send, meta_recv)
     for step in range(1, blocks):
         scatter(step).wait_send()
         gather(step).wait_send()
-    for turn in range(NBATCH):
+    for source in range(blocks):
+        right, left = pieces(source)
+        pl.when(has_right)(right.wait_send)
+        pl.when(has_left)(left.wait_send)
+    for turn in range(1, NBATCH):
         strips_sent(near.at[turn], halo_send.at[turn], halo_recv.at[turn])
 
 
@@ -369,9 +459,11 @@
             jax.ShapeDtypeStruct((near_obs, wide), BF16),
             jax.ShapeDtypeStruct((2 * members, near_obs), BF16),
             jax.ShapeDtypeStruct((near_obs, cells), F32),
+            jax.ShapeDtypeStruct((2 * members, wide), BF16),
+            jax.ShapeDtypeStruct((8, LANES), F32),
         ),
         in_specs=[any_space] * 9,
-        out_specs=[vmem] * 4,
+        out_specs=[vmem] * 6,
         scratch_shapes=[
             pltpu.VMEM((flat, rows), F32),
             pltpu.VMEM((NBATCH, 3, members, wide), F32),
@@ -379,6 +471,7 @@
             pltpu.VMEM((near_obs, wide), F32),
             pltpu.VMEM((members, wide), F32),
             pltpu.VMEM((blocks, members // blocks, wide), F32),
+            pltpu.VMEM((8, wide), F32),
             pltpu.VMEM((5, 1, obs), jnp.int32),
             pltpu.VMEM((2, 1, obs), F32),
             pltpu.SMEM((blocks,), jnp.int32),
@@ -393,6 +486,8 @@
             pltpu.SemaphoreType.DMA((blocks,)),
             pltpu.SemaphoreType.DMA((NBATCH, 2)),
             pltpu.SemaphoreType.DMA((NBATCH, 2)),
+            pltpu.SemaphoreType.DMA((2, blocks)),
+            pltpu.SemaphoreType.DMA((2, blocks)),
         ],
         compiler_params=pltpu.CompilerParams(
             collective_id=0, has_side_effects=True, vmem_limit_bytes=VMEM_LIMIT * 2**20
@@ -406,9 +501,9 @@
         in_hbm(band_reach),
     )
     out = pl.pallas_call(
-        functools.partial(finish, (fields, members, cols, rows)),
+        functools.partial(finish, (fields, members, cols, rows, obs)),
         out_shape=jax.ShapeDtypeStruct((flat, rows), F32),
-        in_specs=[vmem] * 4,
+        in_specs=[vmem] * 6,
         out_specs=any_space,
         scratch_shapes=[pltpu.VMEM((flat, rows), F32), pltpu.SemaphoreType.DMA((fields,))],
         compiler_params=pltpu.CompilerParams(vmem_limit_bytes=VMEM_LIMIT * 2**20),

time: 40.4 us -> 38.7 us (0.958)
  Pallas kernels: 40.2 us -> 38.4 us
    pallas_call x1, Pallas kernels: 37.4 us -> 36.3 us  [shards(): pl.pallas_call(functools.partial(kernel, sizes), out_shape=(jax.ShapeDtyp...]
    pallas_call x1, Pallas kernels: 2.88 us -> 2.1 us  [shards(): pl.pallas_call(functools.partial(finish, (fields, members, cols, rows, ob...]
where the time goes in v4:
time: 38.7 us; the launch traced here: 38.4 us
  Pallas kernels  38.4 us (99%)
    pallas_call x1, Pallas kernels, shards(): pl.pallas_call(functools.partial(kernel, sizes), out_shape=(jax.ShapeDtyp...  36.3 us
    pallas_call x1, Pallas kernels, shards(): pl.pallas_call(functools.partial(finish, (fields, members, cols, rows, ob...  2.1 us

profile of v4, /device:TPU:256, one launch (start us, length us, event | category | flops | bytes accessed | tf_op | source)
XLA Modules:
  0.0 38.4 jit_solution(14820820185772461012)
XLA Ops:
  0.0 36.3 %shard_map.91 = (f32[5,64,512]{2,1,0:T(8,128)S(1)}, bf16[640,256]{1,0:T(8,128)(2,1)S(1)}, bf16[128,640]{1,0:T(8,128)(2,1)S(1)}, f32[640,512]{1,0:T(8,128)S(1)}, ...) custom-call(f32[1280,128]{1,0:T(8,128)} %bitcast.9, s32[1,208]{1,0:T(1,128)} %bitcast.10, s32[1,208]{1,0:T(1,128)} %bitcast.11, ...), custom_call_target="tpu_custom_call" | custom-call | tf_op jit(solution)/shard_map/pallas_call | solution.py:455
  36.3 2.1 %shard_map.92 = f32[1280,128]{1,0:T(8,128)} custom-call(f32[5,64,512]{2,1,0:T(8,128)S(1)} %get-tuple-element.11.state, bf16[640,256]{1,0:T(8,128)(2,1)S(1)} %get-tuple-element.12.dev_t, bf16[128,640]{1,0:T(8,128)(2,1)S(1)} %get-tuple-element.13.factor, f32[640,512]{1,0:T(8,128)S(1)} %get-tuple-element.14.taper_state, ...), custom_call_target="tpu_custom_call" | custom-call | tf_op jit(solution)/shard_map/pallas_call | solution.py:503

commit v5 on v4

--- a/solution.py
+++ b/solution.py
@@ -65,7 +65,7 @@
 
     def run(dev, pull, taper):
         copies = []
-        for group in groups(fields):
+        for group in [list(range(fields))]:
             done = update_fields([state[f] for f in group], dev, pull, taper)
             for f, x in zip(group, done):
                 for c in range(cols):
@@ -243,9 +243,9 @@
 
     own_col, own_row, own_level, own_field = (meta[1, i : i + 1, :] for i in range(4))
     here = (own_level == level.astype(F32)) & (meta[1, 4:5, :] > 0)
-    place = (own_field * cols + own_col - (tile * cols).astype(F32)) * rows + own_row
-    place = jnp.where(here, place, -1.0)
+    place = jnp.where(here, (own_col - (tile * cols).astype(F32)) * rows + own_row, -1.0)
     cell_at = lax.broadcasted_iota(jnp.int32, (cells, wide), 0).astype(F32)
+    chosen = jnp.where(cell_at == place, 1.0, 0.0).astype(BF16)
 
     def slab(ref, f):
         return jnp.concatenate(
@@ -253,14 +253,17 @@
         )
 
     total = jnp.zeros((3 * members, wide), F32)
-    for f in range(fields):
-        loads[f].wait()
-        x = slab(x_in, f)
-        high = x.astype(BF16)
-        rest = x - high.astype(F32)
-        middle, low = split(rest)
-        chosen = jnp.where(cell_at + float(f * cells) == place, 1.0, 0.0).astype(BF16)
-        total = total + dot(jnp.concatenate([high, middle, low], axis=0), chosen)
+    for group in [list(range(fields))]:
+        terms = []
+        for f in group:
+            loads[f].wait()
+            x = slab(x_in, f)
+            high = x.astype(BF16)
+            terms += [high, *split(x - high.astype(F32))]
+        found = dot(jnp.concatenate(terms, axis=0), chosen)
+        for i, f in enumerate(group):
+            part = found[i * 3 * members : (i + 1) * 3 * members]
+            total = jnp.where(own_field == float(f), part, total)
     picked[...] = total[:members] + total[members : 2 * members] + total[2 * members :]
 
     def scatter(step):
@@ -394,7 +397,7 @@
             spread = jnp.sum(deviation * deviation, axis=0, keepdims=True) * (1.0 / (members - 1)) + error
             shrink = 1.0 / (1.0 + jnp.sqrt(error / spread))
             innovation = meta[s, 5:6, :] - average
-            coefficient = jnp.where(flag == float(turn + 1), 1.0 / (spread * (members - 1)), 0.0)
+            coefficient = jnp.where(flag == jnp.asarray(turn + 1, F32), 1.0 / (spread * (members - 1)), 0.0)
             weighted = deviation * coefficient
             turned = jnp.transpose(jnp.concatenate([weighted, weighted], axis=0))
             high = turned.astype(BF16).astype(F32)
@@ -402,30 +405,34 @@
             dev_t[s * obs : (s + 1) * obs] = jnp.concatenate([both, both], axis=1)
             pulls.append((innovation - shrink * deviation)[:, :obs])
         factor[...] = side_by_side(pulls, near_obs)
-        if turn + 1 == NBATCH:
-            short_factor[...] = side_by_side([pull[:, :SHORT] for pull in pulls], wide)
-            counts = [
-                jnp.sum(jnp.where(meta[s, 4:5, :] == float(NBATCH), 1.0, 0.0), axis=1, keepdims=True)
-                for s in range(3)
-            ]
-            most[...] = jnp.broadcast_to(functools.reduce(jnp.maximum, counts), (8, LANES))
-
-    for turn in range(NBATCH):
-        if turn:
-            strips_arrive(near.at[turn], halo_send.at[turn], halo_recv.at[turn])
-        else:
-            for source in range(blocks):
-                right, left = pieces(source)
-                pl.when(has_left)(right.wait_recv)
-                pl.when(has_right)(left.wait_recv)
+        return pulls
+
+    for f in range(fields):
+        state[f] = slab(x_in, f)
+    for source in range(blocks):
+        right, left = pieces(source)
+        pl.when(has_left)(right.wait_recv)
+        pl.when(has_right)(left.wait_recv)
+
+    def batch(turn, carry):
         statistics(turn)
-        if turn + 1 < NBATCH:
-            near[turn + 1, 1] = update(near[turn, 1], dev_t, factor, taper_obs[...])
-            strips_start(near.at[turn + 1], halo_send.at[turn + 1], halo_recv.at[turn + 1])
-            for group in groups(fields):
-                xs = [slab(x_in, f) if turn == 0 else state[f] for f in group]
-                for f, x in zip(group, update_fields(xs, dev_t, factor, taper_state[...])):
-                    state[f] = x
+        near[turn + 1, 1] = update(near[turn, 1], dev_t, factor, taper_obs[...])
+        strips_start(near.at[turn + 1], halo_send.at[turn + 1], halo_recv.at[turn + 1])
+        for group in groups(fields):
+            xs = [state[f] for f in group]
+            for f, x in zip(group, update_fields(xs, dev_t, factor, taper_state[...])):
+                state[f] = x
+        strips_arrive(near.at[turn + 1], halo_send.at[turn + 1], halo_recv.at[turn + 1])
+        return carry
+
+    lax.fori_loop(0, NBATCH - 1, batch, 0)
+    pulls = statistics(NBATCH - 1)
+    short_factor[...] = side_by_side([pull[:, :SHORT] for pull in pulls], wide)
+    counts = [
+        jnp.sum(jnp.where(meta[s, 4:5, :] == float(NBATCH), 1.0, 0.0), axis=1, keepdims=True)
+        for s in range(3)
+    ]
+    most[...] = jnp.broadcast_to(functools.reduce(jnp.maximum, counts), (8, LANES))
 
     strips_sent(meta, meta_send, meta_recv)
     for step in range(1, blocks):

time: 38.7 us -> 38.1 us (0.984)
  Pallas kernels: 38.4 us -> 38 us
where the time goes in v5:
time: 38.1 us; the launch traced here: 38 us
  Pallas kernels  38 us (100%)
    pallas_call x1, Pallas kernels, shards(): pl.pallas_call(functools.partial(kernel, sizes), out_shape=(jax.ShapeDtyp...  36.2 us
    pallas_call x1, Pallas kernels, shards(): pl.pallas_call(functools.partial(finish, (fields, members, cols, rows, ob...  1.83 us

profile of v5, /device:TPU:256, one launch (start us, length us, event | category | flops | bytes accessed | tf_op | source)
XLA Modules:
  0.0 38.0 jit_solution(596095759629170312)
XLA Ops:
  0.0 36.2 %shard_map.91 = (f32[5,64,512]{2,1,0:T(8,128)S(1)}, bf16[640,256]{1,0:T(8,128)(2,1)S(1)}, bf16[128,640]{1,0:T(8,128)(2,1)S(1)}, f32[640,512]{1,0:T(8,128)S(1)}, ...) custom-call(f32[1280,128]{1,0:T(8,128)} %bitcast.9, s32[1,208]{1,0:T(1,128)} %bitcast.10, s32[1,208]{1,0:T(1,128)} %bitcast.11, ...), custom_call_target="tpu_custom_call" | custom-call | tf_op jit(solution)/shard_map/pallas_call | solution.py:462
  36.2 1.8 %shard_map.92 = f32[1280,128]{1,0:T(8,128)} custom-call(f32[5,64,512]{2,1,0:T(8,128)S(1)} %get-tuple-element.11.state, bf16[640,256]{1,0:T(8,128)(2,1)S(1)} %get-tuple-element.12.dev_t, bf16[128,640]{1,0:T(8,128)(2,1)S(1)} %get-tuple-element.13.factor, f32[640,512]{1,0:T(8,128)S(1)} %get-tuple-element.14.taper_state, ...), custom_call_target="tpu_custom_call" | custom-call | tf_op jit(solution)/shard_map/pallas_call | solution.py:510

commit v6 on v5

--- a/solution.py
+++ b/solution.py
@@ -48,13 +48,6 @@
     return x + (both[:members] + both[members:] + dot(factor[:members], gain_low))
 
 
-def update_fields(xs, dev_t, factor, taper):
-    taper = jnp.concatenate([taper] * len(xs), axis=1)
-    x = update(jnp.concatenate(xs, axis=1), dev_t, factor, taper)
-    cells = x.shape[1] // len(xs)
-    return [x[:, i * cells : (i + 1) * cells] for i in range(len(xs))]
-
-
 def groups(fields):
     return [list(range(f, min(f + 2, fields))) for f in range(0, fields, 2)]
 
@@ -64,15 +57,18 @@
     flat = members * cols
 
     def run(dev, pull, taper):
+        taper = jnp.concatenate(
+            [taper[:, c * rows : (c + 1) * rows] for c in range(cols) for f in range(fields)], axis=1
+        )
+        x = update(state[...], dev, pull, taper)
         copies = []
-        for group in [list(range(fields))]:
-            done = update_fields([state[f] for f in group], dev, pull, taper)
-            for f, x in zip(group, done):
-                for c in range(cols):
-                    out[pl.ds(f * flat + c, members, stride=cols), :] = x[:, c * rows : (c + 1) * rows]
-                part = pl.ds(f * flat, flat)
-                copies.append(pltpu.make_async_copy(out.at[part], out_hbm.at[part], out_sem.at[f]))
-                copies[-1].start()
+        for f in range(fields):
+            for c in range(cols):
+                at = (c * fields + f) * rows
+                out[pl.ds(f * flat + c, members, stride=cols), :] = x[:, at : at + rows]
+            part = pl.ds(f * flat, flat)
+            copies.append(pltpu.make_async_copy(out.at[part], out_hbm.at[part], out_sem.at[f]))
+            copies[-1].start()
         for copy in copies:
             copy.wait()
 
@@ -115,6 +111,7 @@
     taper_obs,
     picked,
     parts,
+    right_factor,
     drawn,
     places,
     values,
@@ -136,6 +133,10 @@
     tiles, blocks, fields, members, cols, rows, obs, wide = sizes
     near_obs = dev_t.shape[0]
     cells = cols * rows
+
+    def block(s):
+        return slice(s * obs, (s + 1) * obs)
+
     share = members // blocks
     tile = lax.axis_index("tile")
     level = lax.axis_index("blk")
@@ -330,7 +331,7 @@
         for c in range(cols):
             across = col - (tile * cols + c).astype(F32)
             close = jnp.maximum(1.0 - (across * across + gap) * (1.0 / (cols * cols)), 0.0)
-            taper_state[s * obs : (s + 1) * obs, c * rows : (c + 1) * rows] = close * close * vertical
+            taper_state[block(s), c * rows : (c + 1) * rows] = close * close * vertical
 
     for step in range(1, blocks):
         scatter(step).wait_recv()
@@ -378,7 +379,7 @@
         gap = row - own_row
         close = jnp.maximum(1.0 - (across * across + gap * gap) * (1.0 / (cols * cols)), 0.0)
         vertical = jnp.maximum(0.0, 1.0 - jnp.abs(own_level - lev) * reach_own)
-        taper_obs[s * obs : (s + 1) * obs] = close * close * vertical
+        taper_obs[block(s)] = close * close * vertical
 
     for step in (1, 7, 2, 6, 3, 5, 4):
         gather_arrive(step)
@@ -386,47 +387,60 @@
 
     first_half = lax.broadcasted_iota(jnp.int32, (wide, LANES), 1) < members
 
-    def statistics(turn):
-        pulls = []
-        for s in range(3):
-            prior = near[turn, s]
-            average = jnp.sum(prior, axis=0, keepdims=True) * (1.0 / members)
-            deviation = prior - average
-            flag = meta[s, 4:5, :]
-            error = jnp.where(flag > 0, meta[s, 6:7, :], 1.0)
-            spread = jnp.sum(deviation * deviation, axis=0, keepdims=True) * (1.0 / (members - 1)) + error
-            shrink = 1.0 / (1.0 + jnp.sqrt(error / spread))
-            innovation = meta[s, 5:6, :] - average
-            coefficient = jnp.where(flag == jnp.asarray(turn + 1, F32), 1.0 / (spread * (members - 1)), 0.0)
-            weighted = deviation * coefficient
-            turned = jnp.transpose(jnp.concatenate([weighted, weighted], axis=0))
-            high = turned.astype(BF16).astype(F32)
-            both = jnp.where(first_half, high, turned - high).astype(BF16)[:obs]
-            dev_t[s * obs : (s + 1) * obs] = jnp.concatenate([both, both], axis=1)
-            pulls.append((innovation - shrink * deviation)[:, :obs])
-        factor[...] = side_by_side(pulls, near_obs)
-        return pulls
-
-    for f in range(fields):
-        state[f] = slab(x_in, f)
+    def statistics(turn, s):
+        prior = near[turn, s]
+        average = jnp.sum(prior, axis=0, keepdims=True) * (1.0 / members)
+        deviation = prior - average
+        flag = meta[s, 4:5, :]
+        error = jnp.where(flag > 0, meta[s, 6:7, :], 1.0)
+        spread = jnp.sum(deviation * deviation, axis=0, keepdims=True) * (1.0 / (members - 1)) + error
+        shrink = 1.0 / (1.0 + jnp.sqrt(error / spread))
+        innovation = meta[s, 5:6, :] - average
+        coefficient = jnp.where(flag == jnp.asarray(turn + 1, F32), 1.0 / (spread * (members - 1)), 0.0)
+        weighted = deviation * coefficient
+        turned = jnp.transpose(jnp.concatenate([weighted, weighted], axis=0))
+        high = turned.astype(BF16).astype(F32)
+        both = jnp.where(first_half, high, turned - high).astype(BF16)[:obs]
+        dev_t[block(s)] = jnp.concatenate([both, both], axis=1)
+        return innovation - shrink * deviation
+
+    for c in range(cols):
+        for f in range(fields):
+            state[:, (c * fields + f) * rows : (c * fields + f + 1) * rows] = x_in[
+                pl.ds(f * members * cols + c, members, stride=cols), :
+            ]
     for source in range(blocks):
         right, left = pieces(source)
         pl.when(has_left)(right.wait_recv)
         pl.when(has_right)(left.wait_recv)
 
     def batch(turn, carry):
-        statistics(turn)
+        pulls = [statistics(turn, s)[:, :obs] for s in range(3)]
+        factor[...] = side_by_side(pulls, near_obs)
         near[turn + 1, 1] = update(near[turn, 1], dev_t, factor, taper_obs[...])
         strips_start(near.at[turn + 1], halo_send.at[turn + 1], halo_recv.at[turn + 1])
-        for group in groups(fields):
-            xs = [state[f] for f in group]
-            for f, x in zip(group, update_fields(xs, dev_t, factor, taper_state[...])):
-                state[f] = x
+        right_factor[...] = side_by_side(pulls[1:], near_obs - obs)
+        for first, last, begin, end, pull in (
+            (0, 1, 0, 2 * obs, factor[:, : 2 * obs]),
+            (1, cols - 1, 0, near_obs, factor),
+            (cols - 1, cols, obs, near_obs, right_factor),
+        ):
+            at = slice(first * fields * rows, last * fields * rows)
+            taper = jnp.concatenate(
+                [
+                    taper_state[begin:end, c * rows : (c + 1) * rows]
+                    for c in range(first, last)
+                    for f in range(fields)
+                ],
+                axis=1,
+            )
+            state[:, at] = update(state[:, at], dev_t[begin:end], pull, taper)
         strips_arrive(near.at[turn + 1], halo_send.at[turn + 1], halo_recv.at[turn + 1])
         return carry
 
     lax.fori_loop(0, NBATCH - 1, batch, 0)
-    pulls = statistics(NBATCH - 1)
+    pulls = [statistics(NBATCH - 1, s)[:, :obs] for s in range(3)]
+    factor[...] = side_by_side(pulls, near_obs)
     short_factor[...] = side_by_side([pull[:, :SHORT] for pull in pulls], wide)
     counts = [
         jnp.sum(jnp.where(meta[s, 4:5, :] == float(NBATCH), 1.0, 0.0), axis=1, keepdims=True)
@@ -462,7 +476,7 @@
     made = pl.pallas_call(
         functools.partial(kernel, sizes),
         out_shape=(
-            jax.ShapeDtypeStruct((fields, members, cells), F32),
+            jax.ShapeDtypeStruct((members, fields * cells), F32),
             jax.ShapeDtypeStruct((near_obs, wide), BF16),
             jax.ShapeDtypeStruct((2 * members, near_obs), BF16),
             jax.ShapeDtypeStruct((near_obs, cells), F32),
@@ -478,6 +492,7 @@
             pltpu.VMEM((near_obs, wide), F32),
             pltpu.VMEM((members, wide), F32),
             pltpu.VMEM((blocks, members // blocks, wide), F32),
+            pltpu.VMEM((2 * members, near_obs - obs), BF16),
             pltpu.VMEM((8, wide), F32),
             pltpu.VMEM((5, 1, obs), jnp.int32),
             pltpu.VMEM((2, 1, obs), F32),

time: 38.1 us -> 38.2 us (level)
  no operation moved by 1% of the time
where the time goes in v6:
time: 38.2 us; the launch traced here: 38.1 us
  Pallas kernels  38.1 us (100%)
    pallas_call x1, Pallas kernels, shards(): pl.pallas_call(functools.partial(kernel, sizes), out_shape=(jax.ShapeDtyp...  36.2 us
    pallas_call x1, Pallas kernels, shards(): pl.pallas_call(functools.partial(finish, (fields, members, cols, rows, ob...  1.91 us

profile of v6, /device:TPU:256, one launch (start us, length us, event | category | flops | bytes accessed | tf_op | source)
XLA Modules:
  0.0 38.1 jit_solution(3322225284136456660)
XLA Ops:
  0.0 36.2 %shard_map.91 = (f32[64,2560]{1,0:T(8,128)S(1)}, bf16[640,256]{1,0:T(8,128)(2,1)S(1)}, bf16[128,640]{1,0:T(8,128)(2,1)S(1)}, f32[640,512]{1,0:T(8,128)S(1)}, bf1...) custom-call(f32[1280,128]{1,0:T(8,128)} %bitcast.9, s32[1,208]{1,0:T(1,128)} %bitcast.10, s32[1,208]{1,0:T(1,128)} %bitcast.11, ...), custom_call_target="tpu_custom_call" | custom-call | tf_op jit(solution)/shard_map/pallas_call | solution.py:476
  36.2 1.9 %shard_map.92 = f32[1280,128]{1,0:T(8,128)} custom-call(f32[64,2560]{1,0:T(8,128)S(1)} %get-tuple-element.11.state, bf16[640,256]{1,0:T(8,128)(2,1)S(1)} %get-tuple-element.12.dev_t, bf16[128,640]{1,0:T(8,128)(2,1)S(1)} %get-tuple-element.13.factor, f32[640,512]{1,0:T(8,128)S(1)} %get-tuple-element.14.taper_state, ...), custom_call_target="tpu_custom_call" | custom-call | tf_op jit(solution)/shard_map/pallas_call | solution.py:525

commit v7 on v6

--- a/solution.py
+++ b/solution.py
@@ -310,6 +310,42 @@
         scatter(step).start()
     strips_start(meta, meta_send, meta_recv)
 
+    for step in range(1, blocks):
+        scatter(step).wait_recv()
+    summed = picked[mine, :]
+    for step in range(1, blocks):
+        summed = summed + parts[step]
+    near[0, 1, mine, :] = summed
+    for step in (4, 3, 5, 2, 6, 1, 7):
+        gather(step).start()
+
+    def pieces(source):
+        at = pl.ds(pl.multiple_of(source * share, share), share)
+        right = pltpu.make_async_remote_copy(
+            src_ref=near.at[0, 1, at],
+            dst_ref=near.at[0, 0, at],
+            send_sem=piece_send.at[0, source],
+            recv_sem=piece_recv.at[0, source],
+            device_id={"tile": jnp.minimum(tile + 1, tiles - 1)},
+            device_id_type=MESH,
+        )
+        left = pltpu.make_async_remote_copy(
+            src_ref=near.at[0, 1, at],
+            dst_ref=near.at[0, 2, at],
+            send_sem=piece_send.at[1, source],
+            recv_sem=piece_recv.at[1, source],
+            device_id={"tile": jnp.maximum(tile - 1, 0)},
+            device_id_type=MESH,
+        )
+        return right, left
+
+    def piece_start(source):
+        right, left = pieces(source)
+        pl.when(has_right)(right.start)
+        pl.when(has_left)(left.start)
+
+    piece_start(level)
+
     strips_arrive(meta, meta_send, meta_recv)
     reach_copy.wait()
     reach_here = reach_ref[level].astype(F32) + 1.0
@@ -333,41 +369,6 @@
             close = jnp.maximum(1.0 - (across * across + gap) * (1.0 / (cols * cols)), 0.0)
             taper_state[block(s), c * rows : (c + 1) * rows] = close * close * vertical
 
-    for step in range(1, blocks):
-        scatter(step).wait_recv()
-    summed = picked[mine, :]
-    for step in range(1, blocks):
-        summed = summed + parts[step]
-    near[0, 1, mine, :] = summed
-    for step in (4, 3, 5, 2, 6, 1, 7):
-        gather(step).start()
-
-    def pieces(source):
-        at = pl.ds(pl.multiple_of(source * share, share), share)
-        right = pltpu.make_async_remote_copy(
-            src_ref=near.at[0, 1, at],
-            dst_ref=near.at[0, 0, at],
-            send_sem=piece_send.at[0, source],
-            recv_sem=piece_recv.at[0, source],
-            device_id={"tile": jnp.minimum(tile + 1, tiles - 1)},
-            device_id_type=MESH,
-        )
-        left = pltpu.make_async_remote_copy(
-            src_ref=near.at[0, 1, at],
-            dst_ref=near.at[0, 2, at],
-            send_sem=piece_send.at[1, source],
-            recv_sem=piece_recv.at[1, source],
-            device_id={"tile": jnp.maximum(tile - 1, 0)},
-            device_id_type=MESH,
-        )
-        return right, left
-
-    def piece_start(source):
-        right, left = pieces(source)
-        pl.when(has_right)(right.start)
-        pl.when(has_left)(left.start)
-
-    piece_start(level)
 
     reach_own = jnp.zeros((1, wide), F32)
     for k in range(blocks):
@@ -486,7 +487,7 @@
         in_specs=[any_space] * 9,
         out_specs=[vmem] * 6,
         scratch_shapes=[
-            pltpu.VMEM((flat, rows), F32),
+            pltpu.VMEM((flat + 8, rows), F32),
             pltpu.VMEM((NBATCH, 3, members, wide), F32),
             pltpu.VMEM((3, 8, wide), F32),
             pltpu.VMEM((near_obs, wide), F32),
@@ -527,7 +528,7 @@
         out_shape=jax.ShapeDtypeStruct((flat, rows), F32),
         in_specs=[vmem] * 6,
         out_specs=any_space,
-        scratch_shapes=[pltpu.VMEM((flat, rows), F32), pltpu.SemaphoreType.DMA((fields,))],
+        scratch_shapes=[pltpu.VMEM((flat + 8, rows), F32), pltpu.SemaphoreType.DMA((fields,))],
         compiler_params=pltpu.CompilerParams(vmem_limit_bytes=VMEM_LIMIT * 2**20),
     )(*made)
     return out.reshape(levels, fields, members, cols, rows)

time: 38.2 us -> 38.2 us (level)
  no operation moved by 1% of the time
where the time goes in v7:
time: 38.2 us; the launch traced here: 38.1 us
  Pallas kernels  38.1 us (100%)
    pallas_call x1, Pallas kernels, shards(): pl.pallas_call(functools.partial(kernel, sizes), out_shape=(jax.ShapeDtyp...  36.2 us
    pallas_call x1, Pallas kernels, shards(): pl.pallas_call(functools.partial(finish, (fields, members, cols, rows, ob...  1.91 us

profile of v7, /device:TPU:256, one launch (start us, length us, event | category | flops | bytes accessed | tf_op | source)
XLA Modules:
  0.0 38.1 jit_solution(9672508682783791268)
XLA Ops:
  0.0 36.2 %shard_map.91 = (f32[64,2560]{1,0:T(8,128)S(1)}, bf16[640,256]{1,0:T(8,128)(2,1)S(1)}, bf16[128,640]{1,0:T(8,128)(2,1)S(1)}, f32[640,512]{1,0:T(8,128)S(1)}, bf1...) custom-call(f32[1280,128]{1,0:T(8,128)} %bitcast.9, s32[1,208]{1,0:T(1,128)} %bitcast.10, s32[1,208]{1,0:T(1,128)} %bitcast.11, ...), custom_call_target="tpu_custom_call" | custom-call | tf_op jit(solution)/shard_map/pallas_call | solution.py:477
  36.2 1.9 %shard_map.92 = f32[1280,128]{1,0:T(8,128)} custom-call(f32[64,2560]{1,0:T(8,128)S(1)} %get-tuple-element.11.state, bf16[640,256]{1,0:T(8,128)(2,1)S(1)} %get-tuple-element.12.dev_t, bf16[128,640]{1,0:T(8,128)(2,1)S(1)} %get-tuple-element.13.factor, f32[640,512]{1,0:T(8,128)S(1)} %get-tuple-element.14.taper_state, ...), custom_call_target="tpu_custom_call" | custom-call | tf_op jit(solution)/shard_map/pallas_call | solution.py:526
